TPU v7x, 256 devices: a whole 4x4x8 slice. The times are simulated.
256 devices in a mesh: space: 32 (over y, x, core), wave: 8 (over z).
Axes of the slice: x: 4, y: 4, z: 8, core: 2. Of those that a mesh axis runs over, the one named last changes fastest.
Arguments:
- noise: float32 [8, 3, 32768], P(None, None, 'space'), may hold values from -6 to 6
- positions: float32 [3, 32768], P(None, 'space'), may hold values from 0 to 32, as said below
- wave_index: int32 [3, 4096], P(None, 'wave'), may hold values from -16 to 16, as said below
- tile_lists: int32 [256, 8], P('space'), may hold values from 0 to 23, as said below
- tile_counts: int32 [256], P('space'), may hold values from 0 to 8, as said below
Outputs:
- displacement: float32 [8, 3, 32768], P(None, None, 'space')
Inputs may be any that keep to these rules, and one draw needn't show every extreme that they name: `positions`: particle j has x between j // 1024 and j // 1024 + 1, and y and z between 0 and 8. `wave_index`: row 0 holds n_1 from 1 to 16; rows 1 and 2 hold values from -16 to 15. `tile_lists`: A tile's 8 entries are distinct; window indices below 8 name tiles of the slab before, the next 8 tiles of the own slab, the rest tiles of the slab after. `tile_counts`: the counts of the 8 tiles of one slab add up to exactly 32, and in every slab one tile has 8.
All inputs are finite; a program needn't handle non-finite values.
Results may differ from a plain program's by a relative error of at most 0.0003.
Values sent between devices are 32-bit elements; how exact they have to be, the bound alone decides.
A program may use at most 64 MiB of HBM per device.

v0:
```python
import math

import jax
import jax.numpy as jnp
from jax import lax
from jax.sharding import PartitionSpec as P

TILE = 128
KW = 4096
NB_MOST = 8
DEGREE = 3


PRECISE = lax.Precision.HIGHEST
SIDE_CROSS = 8.0
NEAR_SQUARE = 0.36
NEAR_AMP = 0.15
FAR_AMP = 8.0
SPLIT_SQUARE = 64.0
SCREEN = 4.0
SAFETY = 1.25
SPREAD = 100.0
EPSILON = 1e-06


def padded(x, sides, width):
    for axis, dim in sides:
        size, length = (lax.axis_size(axis), x.shape[dim])
        up = [(i, (i + 1) % size) for i in range(size)]
        down = [(j, i) for i, j in up]
        last = lax.slice_in_dim(x, length - width, length, axis=dim)
        initial = lax.slice_in_dim(x, 0, width, axis=dim)
        before = lax.ppermute(last, axis, up)
        after = lax.ppermute(initial, axis, down)
        x = jnp.concatenate([before, x, after], axis=dim)
    return x


def pair_block(target, source, self_flag, live_weight, length_x):
    box_sides = jnp.array([length_x, SIDE_CROSS, SIDE_CROSS], jnp.float32)[:, None, None]
    offset = target[:, None, :] - source[:, :, None]
    offset = offset - box_sides * jnp.floor(offset / box_sides + 0.5)
    distance_sq = jnp.sum(offset * offset, axis=0)
    tile_width = target.shape[1]
    diagonal_mask = jnp.arange(tile_width)[:, None] == jnp.arange(tile_width)[None, :]
    keep_mask = jnp.where(diagonal_mask & self_flag, 0.0, 1.0) * live_weight
    envelope = NEAR_AMP * jnp.exp(-distance_sq / NEAR_SQUARE) * keep_mask
    outer_product = offset[None, :, :, :] * offset[:, None, :, :]
    identity = jnp.eye(3, dtype=jnp.float32)[:, :, None, None]
    pair_matrix = (identity + outer_product / NEAR_SQUARE) * envelope[None, None]
    return jnp.transpose(pair_matrix, (0, 2, 1, 3)).reshape(3 * tile_width, 3 * tile_width)


def wave_terms(indices, length_x):
    box_sides = jnp.array([length_x, SIDE_CROSS, SIDE_CROSS], jnp.float32)[:, None]
    wave_vectors = 2.0 * math.pi * indices.astype(jnp.float32) / box_sides
    wave_square = jnp.sum(wave_vectors * wave_vectors, axis=0)
    scaled_square = wave_square / SPLIT_SQUARE
    weight = (
        FAR_AMP * (1.0 + scaled_square) * jnp.exp(-scaled_square) / (KW * (wave_square + SCREEN))
    )
    unit_waves = wave_vectors / jnp.sqrt(wave_square)
    return (wave_vectors, weight, unit_waves)


def make_phases(positions, wave_vectors):
    phase_angles = (
        positions[0][:, None] * wave_vectors[0][None, :]
        + positions[1][:, None] * wave_vectors[1][None, :]
        + positions[2][:, None] * wave_vectors[2][None, :]
    )
    return jnp.concatenate([jnp.cos(phase_angles), jnp.sin(phase_angles)], axis=1)


def project(factors, weight, unit_waves):
    along_wave = jnp.sum(factors * unit_waves[None, :, None, :], axis=1)
    return weight * (factors - unit_waves[None, :, None, :] * along_wave[:, None])


def chebyshev(lower_bound, upper_bound):
    node_count = DEGREE + 1
    node_angles = (jnp.arange(node_count, dtype=jnp.float32) + 0.5) * (math.pi / node_count)
    samples = jnp.sqrt(
        0.5 * (upper_bound - lower_bound) * jnp.cos(node_angles) + 0.5 * (upper_bound + lower_bound)
    )
    orders = jnp.arange(node_count, dtype=jnp.float32)
    coeffs = (
        2.0
        / node_count
        * jnp.sum(samples[None, :] * jnp.cos(orders[:, None] * node_angles[None, :]), axis=1)
    )
    return coeffs * jnp.where(orders == 0.0, 0.5, 1.0)


def body(noise, positions, wave_index, tile_lists, tile_counts):
    length_x = float(lax.axis_size("space"))
    vectors = noise.shape[0]
    particle_count = positions.shape[1]
    tile_count = particle_count // TILE
    local_waves = wave_index.shape[1]
    window_positions = padded(positions, (("space", 1),), particle_count)
    own_tiles = positions.reshape(3, tile_count, TILE)
    window_tiles = window_positions.reshape(3, 3 * tile_count, TILE)
    wave_vectors, weight, unit_waves = wave_terms(wave_index, length_x)
    phases = make_phases(positions, wave_vectors)
    wave_count = lax.axis_size("wave")
    wave_rank = lax.axis_index("wave")
    slot_share = NB_MOST // wave_count
    slot_ids = wave_rank + wave_count * jnp.arange(slot_share, dtype=jnp.int32)
    sources = jnp.take(tile_lists, slot_ids, axis=1).reshape(-1)
    targets = jnp.repeat(jnp.arange(tile_count, dtype=jnp.int32), slot_share)
    live_mask = (slot_ids[None, :] < tile_counts[:, None]).reshape(-1).astype(jnp.float32)
    pair_count = sources.shape[0]
    target_pos = jnp.transpose(jnp.take(own_tiles, targets, axis=1), (1, 0, 2))
    source_pos = jnp.transpose(jnp.take(window_tiles, sources, axis=1), (1, 0, 2))
    self_flags = sources == tile_count + targets
    matrices = jax.vmap(pair_block, in_axes=(0, 0, 0, 0, None))(
        target_pos, source_pos, self_flags, live_mask, length_x
    )
    target_hot = (targets[:, None] == jnp.arange(tile_count, dtype=jnp.int32)[None, :]).astype(
        jnp.float32
    )

    def mobility(forces):
        window_forces = padded(forces, (("space", 2),), particle_count)
        window_split = window_forces.reshape(vectors, 3, 3 * tile_count, TILE)
        gathered = jnp.take(window_split, sources, axis=2)
        gathered = jnp.transpose(gathered, (2, 0, 1, 3)).reshape(pair_count, vectors, 3 * TILE)
        pushed = jnp.einsum("pvx,pxy->pvy", gathered, matrices, precision=PRECISE)
        near_part = jnp.einsum("pt,pvy->tvy", target_hot, pushed, precision=PRECISE)
        near_part = jnp.transpose(
            near_part.reshape(tile_count, vectors, 3, TILE), (1, 2, 0, 3)
        ).reshape(vectors, 3, particle_count)
        factors = jnp.dot(
            forces.reshape(vectors * 3, particle_count),
            phases,
            precision=PRECISE,
            preferred_element_type=jnp.float32,
        ).reshape(vectors, 3, 2, local_waves)
        weighted = project(lax.psum(factors, "space"), weight, unit_waves)
        far_part = lax.dot_general(
            weighted.reshape(vectors * 3, 2 * local_waves),
            phases,
            (((1,), (1,)), ((), ())),
            precision=PRECISE,
            preferred_element_type=jnp.float32,
        )
        wave_share = near_part + far_part.reshape(vectors, 3, particle_count)
        return forces + lax.psum(wave_share, "wave")

    first_image = mobility(noise)
    first_sum = lax.psum(jnp.sum(first_image * first_image, axis=(1, 2)), "space")
    first_scale = jnp.sqrt(first_sum + EPSILON)
    unit_image = mobility(first_image / first_scale[:, None, None])
    second_sum = lax.psum(jnp.sum(unit_image * unit_image, axis=(1, 2)), "space")
    upper_bound = SAFETY * jnp.max(jnp.sqrt(second_sum))
    second = unit_image * first_scale[:, None, None]
    lower_bound = upper_bound / SPREAD
    coeffs = chebyshev(lower_bound, upper_bound)
    bound_sum = upper_bound + lower_bound
    bound_span = upper_bound - lower_bound
    previous = noise
    current = (2.0 * first_image - bound_sum * noise) / bound_span
    mapped = (2.0 * second - bound_sum * first_image) / bound_span
    running_sum = coeffs[0] * previous + coeffs[1] * current
    for degree_step in range(2, DEGREE + 1):
        following = 2.0 * (2.0 * mapped - bound_sum * current) / bound_span - previous
        running_sum = running_sum + coeffs[degree_step] * following
        if degree_step < DEGREE:
            mapped = mobility(following)
        previous, current = (current, following)
    return running_sum


def solution(mesh):
    in_specs = (
        P(None, None, "space"),
        P(None, "space"),
        P(None, "wave"),
        P("space", None),
        P("space"),
    )
    out_specs = P(None, None, "space")
    return jax.shard_map(body, mesh=mesh, in_specs=in_specs, out_specs=out_specs, check_vma=False)
```

profile of v0, /device:TPU:1, one launch (start us, length us, event | category | flops | bytes accessed | tf_op | source)
XLA Modules:
  0.0 749.8 jit_solution(6164426227134840273)
XLA Ops:
  10.9 4.2 collective-permute-start.1
  17.8 7.6 %fusion.10 = (f32[1024,512]{1,0:T(8,128)S(1)}, f32[1024,512]{1,0:T(8,128)S(1)}) fusion(f32[512]{0:T(512)S(1)} %bitcast.126, f32[1024]{0:T(1024)S(1)} %bitcast.122, f32[512]{0:T(512)S(1)} %bitcast.125, f32[1024]{0:T(1024)S(1)} %bitcast.123, f32[512]{0:T(512)S(1)} %bitcast.124, f32[1024]{0:T(1024)S(1)} %bitcast.121), kind=kLoop, calls=%fused_computation.23 | loop fusion | flops 2621440 | bytes 4212736 | tf_op jit(solution)/shard_map/cos | solution.py:72
  38.9 4.5 multiply_multiply_fusion
  43.4 8.5 %div.93 = f32[8,384,384]{2,1,0:T(8,128)} reshape(f32[8,3,128,3,128]{4,3,2,1,0:T(4,128)} %multiply_multiply_fusion) | data formatting | bytes 9437184 | tf_op jit(solution)/shard_map/vmap()/div | solution.py:50
  57.2 8.5 %mul.382 = f32[8,384,384]{2,1,0:T(8,128)} reshape(f32[8,3,128,3,128]{4,3,2,1,0:T(4,128)} %mul.381) | data formatting | bytes 9437184 | tf_op jit(solution)/shard_map/vmap()/mul | solution.py:50
  65.7 6.5 add_multiply_fusion
  72.3 67.8 %all-reduce.7.cloned.1.call-done = f32[8,3,2,512]{3,0,2,1:T(8,128)} async-done(((f32[8,3,2,512]{3,0,2,1:T(8,128)}), f32[8,3,2,512]{3,0,2,1:T(8,128)}) %all-reduce.7.cloned.1.call-update) | async-done | bytes 98320 | tf_op jit(solution)/shard_map/psum | solution.py:140
  142.5 4.4 fusion.34
  147.1 4.2 fusion.17
  151.4 4.1 fusion.14
  155.5 5.3 copy.39
  160.8 57.4 %all-reduce.9.cloned.1.call-done = f32[8,3,1024]{2,0,1:T(8,128)} async-done(((f32[8,3,1024]{2,0,1:T(8,128)}), f32[8,3,1024]{2,0,1:T(8,128)}) %all-reduce.9.cloned.1.call-update) | async-done | bytes 98320 | tf_op jit(solution)/shard_map/psum | solution.py:149
  219.3 67.9 %psum.58 = f32[8]{0:T(128)S(1)} all-reduce(f32[8]{0:T(128)S(1)} %get-tuple-element.19), channel_id=1, replica_groups=mesh['space'=32,'wave'=8] {'space'}, use_global_device_ids=true, to_apply=%region_6.8 | all-reduce | flops 8 | bytes 64 | tf_op jit(solution)/shard_map/psum | solution.py:152
  287.2 6.4 fusion.28
  294.5 101.7 %all-reduce.11.cloned.1.call-done = f32[8,3,2,512]{3,0,2,1:T(8,128)} async-done(((f32[8,3,2,512]{3,0,2,1:T(8,128)}), f32[8,3,2,512]{3,0,2,1:T(8,128)}) %all-reduce.11.cloned.1.call-update) | async-done | bytes 98320 | tf_op jit(solution)/shard_map/psum | solution.py:140
  398.7 4.4 fusion.32
  403.3 4.2 fusion.20
  407.6 66.9 %all-reduce.13.cloned.1.call-done = f32[8,3,1024]{2,0,1:T(8,128)} async-done(((f32[8,3,1024]{2,0,1:T(8,128)}), f32[8,3,1024]{2,0,1:T(8,128)}) %all-reduce.13.cloned.1.call-update) | async-done | bytes 98320 | tf_op jit(solution)/shard_map/psum | solution.py:149
  475.5 67.8 %psum.61 = f32[8]{0:T(128)S(1)} all-reduce(f32[8]{0:T(128)S(1)} %multiply_reduce_fusion.2), channel_id=1, replica_groups=mesh['space'=32,'wave'=8] {'space'}, use_global_device_ids=true, to_apply=%region_11.13 | all-reduce | flops 8 | bytes 64 | tf_op jit(solution)/shard_map/psum | solution.py:155
  547.2 6.3 fusion.26
  553.9 106.6 %all-reduce.15.cloned.1.call-done = f32[8,3,2,512]{3,0,2,1:T(8,128)} async-done(((f32[8,3,2,512]{3,0,2,1:T(8,128)}), f32[8,3,2,512]{3,0,2,1:T(8,128)}) %all-reduce.15.cloned.1.call-update) | async-done | bytes 98320 | tf_op jit(solution)/shard_map/psum | solution.py:140
  662.9 4.4 fusion.30
  667.5 4.2 fusion.23
  672.4 66.2 %all-reduce.17.cloned.1.call-done = f32[8,3,1024]{2,0,1:T(8,128)} async-done(((f32[8,3,1024]{2,0,1:T(8,128)}), f32[8,3,1024]{2,0,1:T(8,128)}) %all-reduce.17.cloned.1.call-update) | async-done | bytes 98320 | tf_op jit(solution)/shard_map/psum | solution.py:149
  (110 shorter events, 44.2 us)
Async XLA Ops:
  6.5 133.5 %all-reduce.7.cloned.1.call-start = ((), (), s32[]{:S(2)}) async-start(), calls=%async_computation | async-start | bytes 196608 | tf_op jit(solution)/shard_map/psum | solution.py:140
  6.5 25.2 %collective-permute-start.2 = (f32[3,1024]{1,0:T(4,128)}, f32[3,1024]{1,0:T(4,128)S(1)}, u32[]{:S(2)}, u32[]{:S(2)}) collective-permute-start(f32[3,1024]{1,0:T(4,128)} %param.10), channel_id=1, source_target_pairs={{0,8},{8,16},{16,24},{24,32},{32,40},{40,48},{48,56},{56,64},{64,7... | collective-permute-start | bytes 36872 | tf_op jit(solution)/shard_map/ppermute | solution.py:33
  9.1 22.6 %collective-permute-start.3 = (f32[3,1024]{1,0:T(4,128)}, f32[3,1024]{1,0:T(4,128)S(1)}, u32[]{:S(2)}, u32[]{:S(2)}) collective-permute-start(f32[3,1024]{1,0:T(4,128)} %param.10), channel_id=1, source_target_pairs={{8,0},{16,8},{24,16},{32,24},{40,32},{48,40},{56,48},{64,56},{72,6... | collective-permute-start | bytes 36872 | tf_op jit(solution)/shard_map/ppermute | solution.py:34
  9.7 132.1 %collective-permute-start = (f32[8,3,1024]{2,0,1:T(8,128)}, f32[8,3,1024]{2,0,1:T(8,128)S(1)}, u32[]{:S(2)}, u32[]{:S(2)}) collective-permute-start(f32[8,3,1024]{2,0,1:T(8,128)} %param.9), channel_id=1, source_target_pairs={{0,8},{8,16},{16,24},{24,32},{32,40},{40,48},{48,56},{56,64},{64,7... | collective-permute-start | bytes 294920 | tf_op jit(solution)/shard_map/ppermute | solution.py:33
  10.9 131.0 %collective-permute-start.1 = (f32[8,3,1024]{2,0,1:T(8,128)}, f32[8,3,1024]{2,0,1:T(8,128)S(1)}, u32[]{:S(2)}, u32[]{:S(2)}) collective-permute-start(f32[8,3,1024]{2,0,1:T(8,128)} %param.9), channel_id=1, source_target_pairs={{8,0},{16,8},{24,16},{32,24},{40,32},{48,40},{56,48},{64,56},{72,6... | collective-permute-start | bytes 294920 | tf_op jit(solution)/shard_map/ppermute | solution.py:34
  26.7 3.7 copy-start.10
  26.7 4.0 copy-start.11
  26.7 4.1 copy-start.7
  26.7 4.1 copy-start.9
  29.1 3.4 copy-start.8
  29.8 188.4 %all-reduce.9.cloned.1.call-start = ((), (), s32[]{:S(2)}) async-start(), calls=%async_computation.1 | async-start | bytes 196608 | tf_op jit(solution)/shard_map/psum | solution.py:149
  35.9 2.9 copy-start.4
  65.7 76.2 %copy-start.5 = (f32[8,3,1024]{2,0,1:T(8,128)S(1)}, f32[8,3,1024]{2,0,1:T(8,128)}, u32[]{:S(2)}) copy-start(f32[8,3,1024]{2,0,1:T(8,128)} %param.9) | copy-start | bytes 294916
  142.5 4.6 copy-start.1
  151.4 244.9 %all-reduce.11.cloned.1.call-start = ((), (), s32[]{:S(2)}) async-start(), calls=%async_computation.2 | async-start | bytes 196608 | tf_op jit(solution)/shard_map/psum | solution.py:140
  293.6 180.8 %all-reduce.13.cloned.1.call-start = ((), (), s32[]{:S(2)}) async-start(), calls=%async_computation.3 | async-start | bytes 196608 | tf_op jit(solution)/shard_map/psum | solution.py:149
  293.8 104.3 %collective-permute-start.4 = (f32[8,3,1024]{2,0,1:T(8,128)S(1)}, f32[8,3,1024]{2,0,1:T(8,128)S(1)}, u32[]{:S(2)}, u32[]{:S(2)}) collective-permute-start(f32[8,3,1024]{2,0,1:T(8,128)S(1)} %broadcast_divide_fusion), channel_id=1, source_target_pairs={{0,8},{8,16},{16,24},{24,32},{32,40},{40,48},{48,56},{56,64},{64,7... | collective-permute-start | bytes 294920 | tf_op jit(solution)/shard_map/ppermute | solution.py:33
  293.8 104.2 %collective-permute-start.5 = (f32[8,3,1024]{2,0,1:T(8,128)S(1)}, f32[8,3,1024]{2,0,1:T(8,128)S(1)}, u32[]{:S(2)}, u32[]{:S(2)}) collective-permute-start(f32[8,3,1024]{2,0,1:T(8,128)S(1)} %broadcast_divide_fusion), channel_id=1, source_target_pairs={{8,0},{16,8},{24,16},{32,24},{40,32},{48,40},{56,48},{64,56},{72,6... | collective-permute-start | bytes 294920 | tf_op jit(solution)/shard_map/ppermute | solution.py:34
  398.7 4.6 copy-start.2
  407.5 252.9 %all-reduce.15.cloned.1.call-start = ((), (), s32[]{:S(2)}) async-start(), calls=%async_computation.4 | async-start | bytes 196608 | tf_op jit(solution)/shard_map/psum | solution.py:140
  546.2 116.1 %collective-permute-start.6 = (f32[8,3,1024]{2,0,1:T(8,128)S(1)}, f32[8,3,1024]{2,0,1:T(8,128)S(1)}, u32[]{:S(2)}, u32[]{:S(2)}) collective-permute-start(f32[8,3,1024]{2,0,1:T(8,128)S(1)} %divide_subtract_fusion), channel_id=1, source_target_pairs={{0,8},{8,16},{16,24},{24,32},{32,40},{40,48},{48,56},{56,64},{64,7... | collective-permute-start | bytes 294920 | tf_op jit(solution)/shard_map/ppermute | solution.py:33
  546.3 116.0 %collective-permute-start.7 = (f32[8,3,1024]{2,0,1:T(8,128)S(1)}, f32[8,3,1024]{2,0,1:T(8,128)S(1)}, u32[]{:S(2)}, u32[]{:S(2)}) collective-permute-start(f32[8,3,1024]{2,0,1:T(8,128)S(1)} %divide_subtract_fusion), channel_id=1, source_target_pairs={{8,0},{16,8},{24,16},{32,24},{40,32},{48,40},{56,48},{64,56},{72,6... | collective-permute-start | bytes 294920 | tf_op jit(solution)/shard_map/ppermute | solution.py:34
  553.6 185.1 %all-reduce.17.cloned.1.call-start = ((), (), s32[]{:S(2)}) async-start(), calls=%async_computation.5 | async-start | bytes 196608 | tf_op jit(solution)/shard_map/psum | solution.py:149
  662.9 4.6 copy-start.3
  (2 other events, 3.4 us)
Sparse Core Ops, SparseCore 0:
  30.0 110.0 all-reduce.6
  151.5 66.7 all-reduce.8
  293.7 102.4 all-reduce.10
  407.6 66.7 all-reduce.12
  553.7 106.6 all-reduce.14
  671.9 66.7 all-reduce.16
where the time goes:
time: 758 us; the launch traced here: 750 us
  waiting for transfers between devices  467 us (62%)
  blocking collectives  136 us (18%)
  other arithmetic  44.3 us (6%)
  matrix products  41.4 us (5%)
  local copies, waits for them, and re-layouts  35.1 us (5%)
  between operations  15.5 us (2%)
  starting transfers between devices  11.1 us (1%)
    psum x3, waiting for transfers between devices, mobility(): weighted = project(lax.psum(factors, 'space'), weight, unit_waves)  276 us
    psum x3, waiting for transfers between devices, mobility(): return forces + lax.psum(wave_share, 'wave')  191 us
    psum x1, blocking collectives, body(): lax.psum(jnp.sum(first_image * first_image, axis=(1, 2)), 'space')  67.9 us
    psum x1, blocking collectives, body(): lax.psum(jnp.sum(unit_image * unit_image, axis=(1, 2)), 'space')  67.8 us
  transfers between devices with their start and end apart: 14, of which 6 were waited for; matrix products, arithmetic and copies ran while one was open for 10% of the time, Pallas kernels for 0%

commit v1 on v0

v1 whole, which is shorter than its diff:
```python
import functools
import math

import jax
import jax.numpy as jnp
from jax import lax
from jax.experimental import pallas as pl
from jax.experimental.pallas import tpu as pltpu
from jax.sharding import PartitionSpec as P

MESH = pl.DeviceIdType.MESH
F32 = jnp.float32
BF16 = jnp.bfloat16

KW = 4096
DEGREE = 3
TILE = 128
SIDE_CROSS = 8.0
NEAR_SQUARE = 0.36
NEAR_AMP = 0.15
FAR_AMP = 8.0
SPLIT_SQUARE = 64.0
SCREEN = 4.0
SAFETY = 1.25
SPREAD = 100.0
EPSILON = 1e-06

SINE = (6.283185160087367, -41.34165503087954, 81.60100403735636, -76.54978142115317, 39.5366991046531)


def split_rows(x):
    high = x.astype(BF16).astype(F32)
    return jnp.concatenate([high, x - high], axis=0).astype(BF16)


def sine_of_turns(a):
    a2 = a * a
    p = F32(SINE[-1])
    for c in SINE[-2::-1]:
        p = p * a2 + F32(c)
    return p * a


def nearest(x):
    return jnp.floor(x + 0.5)


def kernel(
    n_space,
    n_wave,
    noise_ref,
    pos_ref,
    wave_ref,
    lists_ref,
    counts_ref,
    out_ref,
    ph_hi,
    ph_lo,
    posw,
    ev,
    nf,
    bm_hi,
    bm_lo,
    u,
    near,
    sbuf,
    rs,
    agb,
    vbuf,
    wr,
    nsrc,
    nrecv,
    outb,
    rs_s,
    rs_r,
    ag_s,
    ag_r,
    wr_s,
    wr_r,
    wa_s,
    wa_r,
    halo_s,
    halo_r,
    pos_s,
    pos_r,
    norm_s,
    norm_r,
):
    me = lax.axis_index("space")
    wv = lax.axis_index("wave")
    up = lax.rem(me + 1, n_space)
    down = lax.rem(me + n_space - 1, n_space)
    tiles = n_wave

    barrier = pltpu.get_barrier_semaphore()

    def greet_space(d, _):
        pl.semaphore_signal(
            barrier, inc=1, device_id=(lax.rem(me + d, n_space), wv), device_id_type=MESH
        )
        return 0

    def greet_wave(d, _):
        pl.semaphore_signal(
            barrier, inc=1, device_id=(me, lax.rem(wv + d, n_wave)), device_id_type=MESH
        )
        return 0

    lax.fori_loop(1, n_space, greet_space, 0)
    lax.fori_loop(1, n_wave, greet_wave, 0)

    def remote(src, dst, ssem, rsem, s, w):
        return pltpu.make_async_remote_copy(
            src_ref=src,
            dst_ref=dst,
            send_sem=ssem,
            recv_sem=rsem,
            device_id=(s, w),
            device_id_type=MESH,
        )

    for t in range(tiles):
        lanes = slice(t * TILE, (t + 1) * TILE)
        posw[tiles + t] = jnp.concatenate(
            [pos_ref[:, lanes], jnp.zeros((5, TILE), F32)], axis=0
        )
        u[0, tiles + t] = noise_ref[:, lanes]

    waves = wave_ref.shape[1]
    n_all = wave_ref[...].astype(F32)
    n_rows = [jnp.broadcast_to(n_all[c : c + 1], (8, waves)) for c in range(3)]
    ka = n_rows[0] * F32(2.0 * math.pi / n_space)
    kb = n_rows[1] * F32(2.0 * math.pi / SIDE_CROSS)
    kc = n_rows[2] * F32(2.0 * math.pi / SIDE_CROSS)
    plane = ka * ka + kb * kb
    square = plane + kc * kc
    scaled = square / SPLIT_SQUARE
    weight = FAR_AMP * (1.0 + scaled) * jnp.exp(-scaled) / (KW * (square + SCREEN))
    root = jnp.sqrt(weight)
    rho = jnp.sqrt(plane)
    length = jnp.sqrt(square)
    ev[0] = -root * kb / rho
    ev[1] = root * ka / rho
    ev[2] = -root * ka * kc / (rho * length)
    ev[3] = -root * kb * kc / (rho * length)
    ev[4] = root * rho / length
    for c in range(3):
        nf[c] = n_rows[c]

    def make_phases(t, _):
        cols = jnp.transpose(posw[tiles + t])
        for j in range(TILE // 16):
            rows = pl.ds(pl.multiple_of(t * TILE + j * 16, 16), 16)
            part = cols[j * 16 : (j + 1) * 16]
            tx = part[:, 0:1] * F32(1.0 / n_space)
            ty = part[:, 1:2] * F32(1.0 / SIDE_CROSS)
            tz = part[:, 2:3] * F32(1.0 / SIDE_CROSS)
            turns = tx * nf[0, 0:1] + ty * nf[1, 0:1] + tz * nf[2, 0:1]
            r = turns - nearest(turns)
            q = r - 0.25
            q = q - nearest(q)
            cosine = sine_of_turns(0.25 - jnp.abs(r))
            sine = sine_of_turns(0.25 - jnp.abs(q))
            for at, value in ((0, cosine), (waves, sine)):
                high = value.astype(BF16)
                ph_hi[rows, at : at + waves] = high
                ph_lo[rows, at : at + waves] = (value - high.astype(F32)).astype(BF16)
        return 0

    lax.fori_loop(0, tiles, make_phases, 0)

    def halo(k):
        own = u.at[k, pl.ds(tiles, tiles)]
        return (
            remote(own, u.at[k, pl.ds(0, tiles)], halo_s.at[k, 0], halo_r.at[k, 0], up, wv),
            remote(own, u.at[k, pl.ds(2 * tiles, tiles)], halo_s.at[k, 1], halo_r.at[k, 1], down, wv),
        )

    own_pos = posw.at[pl.ds(tiles, tiles)]
    pos_copies = (
        remote(own_pos, posw.at[pl.ds(0, tiles)], pos_s.at[0], pos_r.at[0], up, wv),
        remote(own_pos, posw.at[pl.ds(2 * tiles, tiles)], pos_s.at[1], pos_r.at[1], down, wv),
    )

    pl.semaphore_wait(barrier, n_space - 1 + n_wave - 1)

    for copy in pos_copies + halo(0):
        copy.start()

    def pair_of(i):
        j = wv * (32 // n_wave) + i
        total = jnp.int32(0)
        tile = jnp.int32(0)
        base = jnp.int32(0)
        for t in range(tiles):
            total = total + counts_ref[t]
            past = total <= j
            tile = tile + past.astype(jnp.int32)
            base = jnp.where(past, total, base)
        tile = jnp.minimum(tile, tiles - 1)
        slot = jnp.clip(j - base, 0, lists_ref.shape[1] - 1)
        return tile, jnp.clip(lists_ref[tile, slot], 0, 3 * tiles - 1)

    pairs = 32 // n_wave

    def build_pair(i, _):
        tile, source = pair_of(i)
        target_rows = posw[tiles + tile]
        source_cols = jnp.transpose(posw[source])
        offs = []
        for c, side in enumerate((float(n_space), SIDE_CROSS, SIDE_CROSS)):
            off = target_rows[c : c + 1] - source_cols[:, c : c + 1]
            offs.append(off - F32(side) * jnp.floor(off * F32(1.0 / side) + 0.5))
        square = offs[0] * offs[0] + offs[1] * offs[1] + offs[2] * offs[2]
        diagonal = lax.broadcasted_iota(jnp.int32, (TILE, TILE), 0) == lax.broadcasted_iota(
            jnp.int32, (TILE, TILE), 1
        )
        own = jnp.where(source == tiles + tile, F32(0.0), F32(1.0))
        keep = jnp.where(diagonal, own, F32(1.0))
        envelope = NEAR_AMP * jnp.exp(-square / NEAR_SQUARE) * keep
        scaled_env = envelope / NEAR_SQUARE
        for a in range(3):
            left = offs[a] * scaled_env
            for b in range(a, 3):
                block = left * offs[b]
                if a == b:
                    block = block + envelope
                high = block.astype(BF16)
                low = (block - high.astype(F32)).astype(BF16)
                for p, q in sorted({(a, b), (b, a)}):
                    at = (i, slice(p * TILE, (p + 1) * TILE), slice(q * TILE, (q + 1) * TILE))
                    bm_hi[at] = high
                    bm_lo[at] = low
        return 0

    def near_apply(k):
        near[...] = jnp.zeros_like(near)

        def one_pair(i, _):
            tile, source = pair_of(i)
            f = u[k, source]
            lhs = split_rows(jnp.concatenate([f[0:8], f[8:16], f[16:24]], axis=1))
            res = jnp.dot(lhs, bm_hi[i], preferred_element_type=F32) + jnp.dot(
                lhs, bm_lo[i], preferred_element_type=F32
            )
            res = res[0:8] + res[8:16]
            res = jnp.concatenate([res[:, c * TILE : (c + 1) * TILE] for c in range(3)], axis=0)
            for t in range(tiles):
                near[t] += jnp.where(tile == t, res, 0.0)
            return 0

        lax.fori_loop(0, pairs, one_pair, 0)

    def send_space(src_of, dst, ssem, rsem):
        def one(d, _):
            peer = lax.rem(me + d, n_space)
            remote(src_of(peer), dst, ssem, rsem, peer, wv).start()
            return 0

        lax.fori_loop(1, n_space, one, 0)

    def all_but_one(ref, count, ssem, rsem):
        some = ref.at[pl.ds(0, count)]
        return remote(some, some, ssem, rsem, up, wv)

    waiting = []
    sent = []

    for k in range(DEGREE):
        x = jnp.concatenate([u[k, tiles + t] for t in range(tiles)], axis=1)
        lhs = split_rows(x)
        step = 256
        for n in range(waves // step):
            parts = []
            for half in range(2):
                cols = slice(half * waves + n * step, half * waves + (n + 1) * step)
                c = jnp.dot(lhs, ph_hi[:, cols], preferred_element_type=F32) + jnp.dot(
                    lhs, ph_lo[:, cols], preferred_element_type=F32
                )
                parts.append(c[0:24] + c[24:48])
            for half in range(2):
                c = parts[half]
                for q in range(step // TILE):
                    lanes = slice(q * TILE, (q + 1) * TILE)
                    at = slice(n * step + q * TILE, n * step + (q + 1) * TILE)
                    c0, c1, c2 = c[0:8, lanes], c[8:16, lanes], c[16:24, lanes]
                    d0 = ev[0, :, at] * c0 + ev[1, :, at] * c1
                    d1 = ev[2, :, at] * c0 + ev[3, :, at] * c1 + ev[4, :, at] * c2
                    chip = half * (waves // TILE) + n * (step // TILE) + q
                    for tangent, d in ((0, d0), (1, d1)):
                        slot = 2 * (tangent * (2 * waves // TILE) + chip)
                        sbuf[k, slot] = d[0:4]
                        sbuf[k, slot + 1] = d[4:8]
        rs[k, me] = sbuf[k, me]
        send_space(lambda peer: sbuf.at[k, peer], rs.at[k, me], rs_s.at[k], rs_r.at[k])
        sent.append((sbuf.at[k], n_space - 1, rs_s.at[k], rs_r.at[k]))

        if k > 0:
            total = jnp.zeros((8, TILE), F32)
            for t in range(tiles):
                v = u[k, tiles + t]
                v = v * v
                total = total + (v[0:8] + v[8:16] + v[16:24])
            lane_sum = jnp.sum(total, axis=1, keepdims=True)
            pick = lax.broadcasted_iota(jnp.int32, (8, TILE), 0) == lax.broadcasted_iota(
                jnp.int32, (8, TILE), 1
            )
            row = jnp.sum(jnp.where(pick, lane_sum, 0.0), axis=0, keepdims=True)
            nsrc[k - 1] = row
            nrecv[k - 1, me] = row
            send_space(
                lambda peer: nsrc.at[k - 1],
                nrecv.at[k - 1, me],
                norm_s.at[k - 1],
                norm_r.at[k - 1],
            )
            sent.append((nrecv.at[k - 1], n_space - 1, norm_s.at[k - 1], norm_r.at[k - 1]))

        if k == 0:
            for copy in pos_copies:
                copy.wait_recv()
            lax.fori_loop(0, pairs, build_pair, 0)
        for copy in halo(k):
            copy.wait_recv()
        near_apply(k)

        all_but_one(rs.at[k], n_space - 1, rs_s.at[k], rs_r.at[k]).wait_recv()
        total = rs[k, 0]
        for s in range(1, n_space):
            total = total + rs[k, s]
        agb[k, me] = total
        send_space(lambda peer: agb.at[k, me], agb.at[k, me], ag_s.at[k], ag_r.at[k])
        sent.append((agb.at[k], n_space - 1, ag_s.at[k], ag_r.at[k]))
        all_but_one(agb.at[k], n_space - 1, ag_s.at[k], ag_r.at[k]).wait_recv()

        rows = [[], [], []]
        for half in range(2):
            for n in range(waves // TILE):
                at = slice(n * TILE, (n + 1) * TILE)
                chip = half * (waves // TILE) + n
                d = []
                for tangent in range(2):
                    slot = 2 * (tangent * (2 * waves // TILE) + chip)
                    d.append(jnp.concatenate([agb[k, slot], agb[k, slot + 1]], axis=0))
                rows[0].append(ev[0, :, at] * d[0] + ev[2, :, at] * d[1])
                rows[1].append(ev[1, :, at] * d[0] + ev[3, :, at] * d[1])
                rows[2].append(ev[4, :, at] * d[1])
        lhs = split_rows(
            jnp.concatenate([jnp.concatenate(r, axis=1) for r in rows], axis=0)
        )
        contract = (((1,), (1,)), ((), ()))
        for n in range(tiles // 2):
            span = slice(n * 2 * TILE, (n + 1) * 2 * TILE)
            v = lax.dot_general(
                lhs, ph_hi[span, :], contract, preferred_element_type=F32
            ) + lax.dot_general(lhs, ph_lo[span, :], contract, preferred_element_type=F32)
            v = v[0:24] + v[24:48]
            for q in range(2):
                t = 2 * n + q
                vbuf[k, t] = v[:, q * TILE : (q + 1) * TILE] + near[t]

        wr[k, wv] = vbuf[k, wv] + u[k, tiles + wv]

        def send_part(d, _):
            peer = lax.rem(wv + d, n_wave)
            remote(vbuf.at[k, peer], wr.at[k, wv], wr_s.at[k], wr_r.at[k], me, peer).start()
            return 0

        lax.fori_loop(1, n_wave, send_part, 0)
        sent.append((wr.at[k], n_wave - 1, wr_s.at[k], wr_r.at[k]))
        all_but_one(wr.at[k], n_wave - 1, wr_s.at[k], wr_r.at[k]).wait_recv()
        image = wr[k, 0]
        for w in range(1, n_wave):
            image = image + wr[k, w]

        if k < DEGREE - 1:
            own = u.at[k + 1, tiles + wv]
            u[k + 1, tiles + wv] = image
            whole = u.at[k + 1, pl.ds(tiles, tiles)]
        else:
            for j in range(2):
                all_but_one(nrecv.at[j], n_space - 1, norm_s.at[j], norm_r.at[j]).wait_recv()
            sums = []
            for j in range(2):
                total = nrecv[j, 0]
                for s in range(1, n_space):
                    total = total + nrecv[j, s]
                sums.append(total)
            ratio = jnp.max(sums[1] / (sums[0] + EPSILON), axis=1, keepdims=True)
            high = SAFETY * jnp.sqrt(jnp.broadcast_to(ratio, (8, TILE)))
            low = high / SPREAD
            nodes = DEGREE + 1
            angles = [(j + 0.5) * math.pi / nodes for j in range(nodes)]
            samples = [
                jnp.sqrt(0.5 * (high - low) * F32(math.cos(a)) + 0.5 * (high + low)) for a in angles
            ]
            coeffs = []
            for order in range(nodes):
                c = samples[0] * F32(math.cos(order * angles[0]))
                for j in range(1, nodes):
                    c = c + samples[j] * F32(math.cos(order * angles[j]))
                coeffs.append(c * F32((1.0 if order == 0 else 2.0) / nodes))
            bound_sum = high + low
            scale = 1.0 / (high - low)
            pieces = []
            for c in range(3):
                at = slice(c * 8, (c + 1) * 8)
                f = u[0, tiles + wv, at]
                u1 = u[1, tiles + wv, at]
                u2 = u[2, tiles + wv, at]
                u3 = image[at]
                t1 = (2.0 * u1 - bound_sum * f) * scale
                mt1 = (2.0 * u2 - bound_sum * u1) * scale
                mmt1 = (2.0 * u3 - bound_sum * u2) * scale
                t2 = 2.0 * (2.0 * mt1 - bound_sum * t1) * scale - f
                mt2 = 2.0 * (2.0 * mmt1 - bound_sum * mt1) * scale - u1
                t3 = 2.0 * (2.0 * mt2 - bound_sum * t2) * scale - t1
                pieces.append(coeffs[0] * f + coeffs[1] * t1 + coeffs[2] * t2 + coeffs[3] * t3)
            own = outb.at[wv]
            outb[wv] = jnp.concatenate(pieces, axis=0)
            whole = outb

        def send_tile(d, _):
            remote(own, own, wa_s.at[k], wa_r.at[k], me, lax.rem(wv + d, n_wave)).start()
            return 0

        lax.fori_loop(1, n_wave, send_tile, 0)
        sent.append((whole, n_wave - 1, wa_s.at[k], wa_r.at[k]))
        all_but_one(whole, n_wave - 1, wa_s.at[k], wa_r.at[k]).wait_recv()
        if k < DEGREE - 1:
            for copy in halo(k + 1):
                copy.start()

    out_ref[...] = outb[...]
    for ref, count, ssem, rsem in sent:
        all_but_one(ref, count, ssem, rsem).wait_send()
    for copy in pos_copies:
        copy.wait_send()
    for k in range(DEGREE):
        for copy in halo(k):
            copy.wait_send()


def body(n_space, n_wave, noise, positions, wave_index, tile_lists, tile_counts):
    tiles = positions.shape[1] // TILE
    count = positions.shape[1]
    waves = wave_index.shape[1]
    vectors = noise.shape[0]
    rows = vectors * 3
    arranged = jnp.transpose(noise, (1, 0, 2)).reshape(rows, count)
    pairs = 32 // n_wave
    vmem = pl.BlockSpec(memory_space=pltpu.VMEM)
    smem = pl.BlockSpec(memory_space=pltpu.SMEM)
    dma = pltpu.SemaphoreType.DMA

    out = pl.pallas_call(
        functools.partial(kernel, n_space, n_wave),
        out_shape=jax.ShapeDtypeStruct((tiles, rows, TILE), F32),
        in_specs=[vmem, vmem, vmem, smem, smem],
        out_specs=vmem,
        scratch_shapes=[
            pltpu.VMEM((count, 2 * waves), BF16),
            pltpu.VMEM((count, 2 * waves), BF16),
            pltpu.VMEM((3 * tiles, 8, TILE), F32),
            pltpu.VMEM((5, 8, waves), F32),
            pltpu.VMEM((3, 8, waves), F32),
            pltpu.VMEM((pairs, 3 * TILE, 3 * TILE), BF16),
            pltpu.VMEM((pairs, 3 * TILE, 3 * TILE), BF16),
            pltpu.VMEM((DEGREE, 3 * tiles, rows, TILE), F32),
            pltpu.VMEM((tiles, rows, TILE), F32),
            pltpu.VMEM((DEGREE, n_space, 4, TILE), F32),
            pltpu.VMEM((DEGREE, n_space, 4, TILE), F32),
            pltpu.VMEM((DEGREE, n_space, 4, TILE), F32),
            pltpu.VMEM((DEGREE, tiles, rows, TILE), F32),
            pltpu.VMEM((DEGREE, tiles, rows, TILE), F32),
            pltpu.VMEM((2, 1, TILE), F32),
            pltpu.VMEM((2, n_space, 1, TILE), F32),
            pltpu.VMEM((tiles, rows, TILE), F32),
            dma((DEGREE,)),
            dma((DEGREE,)),
            dma((DEGREE,)),
            dma((DEGREE,)),
            dma((DEGREE,)),
            dma((DEGREE,)),
            dma((DEGREE,)),
            dma((DEGREE,)),
            dma((DEGREE, 2)),
            dma((DEGREE, 2)),
            dma((2,)),
            dma((2,)),
            dma((2,)),
            dma((2,)),
        ],
        compiler_params=pltpu.CompilerParams(
            collective_id=0, has_side_effects=True, vmem_limit_bytes=32 * 1024 * 1024
        ),
    )(arranged, positions, wave_index, tile_lists, tile_counts)
    out = out.reshape(tiles, 3, vectors, TILE)
    return jnp.transpose(out, (2, 1, 0, 3)).reshape(vectors, 3, count)


def solution(mesh):
    n_space, n_wave = mesh.shape["space"], mesh.shape["wave"]

    def step(*args):
        return body(n_space, n_wave, *args)

    in_specs = (
        P(None, None, "space"),
        P(None, "space"),
        P(None, "wave"),
        P("space", None),
        P("space"),
    )
    out_specs = P(None, None, "space")
    return jax.shard_map(step, mesh=mesh, in_specs=in_specs, out_specs=out_specs, check_vma=False)
```

time: 758 us -> 84.2 us (0.11); the launches traced: 750 us -> 84 us
  waiting for transfers between devices: 467 us -> 0 us
  blocking collectives: 136 us -> 0 us
  Pallas kernels: 0 us -> 79.7 us
  other arithmetic: 44.3 us -> 0 us
  matrix products: 41.4 us -> 0 us
  local copies, waits for them, and re-layouts: 35.1 us -> 4.29 us
  between operations: 15.5 us -> 0.01 us
  starting transfers between devices: 11.1 us -> 0 us
    psum x6 -> x0, waiting for transfers between devices: 467 us -> none  [the longest x3 276 us: mobility(): weighted = project(lax.psum(factors, 'space'), weight, unit_waves)]
    psum x2 -> x0, blocking collectives: 136 us -> none  [the longest x1 67.9 us: body(): lax.psum(jnp.sum(first_image * first_image, axis=(1, 2)), 'space')]
    pallas_call x0 -> x1, Pallas kernels: none -> 79.7 us  [body(): pl.pallas_call(functools.partial(kernel, n_space, n_wave), out_shape=jax....]
    dot_general x12 -> x0, matrix products: 41.4 us -> none  [the longest x3 15 us: mobility(): jnp.dot(forces.reshape(vectors * 3, particle_count), phases, precision=PR...]
    mul x2 -> x0, local copies, waits for them, and re-layouts: 12.6 us -> none  [pair_block(): (identity + outer_product / NEAR_SQUARE) * envelope[None, None]]
    mul x7 -> x0, other arithmetic: 10.5 us -> none  [the longest x1 6.54 us: pair_block(): (identity + outer_product / NEAR_SQUARE) * envelope[None, None]]
    ppermute x8 -> x0, starting transfers between devices: 10.3 us -> none  [the longest x4 6.48 us: padded(): after = lax.ppermute(initial, axis, down)]
    div x1 -> x0, local copies, waits for them, and re-layouts: 8.52 us -> none  [pair_block(): outer_product / NEAR_SQUARE]
  transfers between devices with their start and end apart: 14 -> 0, of which waited for: 6 -> 0; matrix products, arithmetic and copies ran while one was open for 10% -> 0% of each run, Pallas kernels for 0% -> 0%
where the time goes in v1:
time: 84.2 us; the launch traced here: 84 us
  Pallas kernels  79.7 us (95%)
  local copies, waits for them, and re-layouts  4.29 us (5%)
    pallas_call x1, Pallas kernels, body(): pl.pallas_call(functools.partial(kernel, n_space, n_wave), out_shape=jax....  79.7 us
    unnamed x10, local copies, waits for them, and re-layouts  3.65 us

profile of v1, /device:TPU:1, one launch (start us, length us, event | category | flops | bytes accessed | tf_op | source)
XLA Modules:
  0.0 84.0 jit_solution(5895640206648859963)
XLA Ops:
  0.0 0.0 copy-start.4
  0.0 0.7 copy-done.4
  0.7 0.0 copy-start
  0.7 0.9 %copy-done = f32[8,3,1024]{2,0,1:T(8,128)S(1)} copy-done((f32[8,3,1024]{2,0,1:T(8,128)S(1)}, f32[8,3,1024]{2,0,1:T(8,128)}, u32[]{:S(2)}) %copy-start) | copy-done | bytes 98328
  1.5 0.0 copy-start.1
  1.6 0.7 copy-done.1
  2.3 0.0 copy-start.2
  2.3 0.7 copy-done.2
  3.0 0.0 copy-start.3
  3.0 0.7 copy-done.3
  3.7 79.7 %shard_map.55 = f32[8,24,128]{2,1,0:T(8,128)S(1)} custom-call(f32[24,1024]{1,0:T(8,128)S(1)} %bitcast.10, f32[3,1024]{1,0:T(4,128)S(1)} %copy-done.1, s32[3,512]{1,0:T(4,128)S(1)} %copy-done.2, s32[8,8]{1,0:T(8,128)S(1)} %copy-done.3, s32[8]{0:T(128)S(1)} %copy-done.4), custom_call_target="tpu_custom_call" | custom-call | tf_op jit(solution)/shard_map/pallas_call | solution.py:456
  83.3 0.6 copy_bitcast_fusion
Async XLA Ops:
  0.0 0.7 copy-start.4
  0.7 0.9 %copy-start = (f32[8,3,1024]{2,0,1:T(8,128)S(1)}, f32[8,3,1024]{2,0,1:T(8,128)}, u32[]{:S(2)}) copy-start(f32[8,3,1024]{2,0,1:T(8,128)} %param.5) | copy-start | bytes 294916
  1.5 0.7 copy-start.1
  2.3 0.7 copy-start.2
  3.0 0.7 copy-start.3

commit v2 on v1

--- a/solution.py
+++ b/solution.py
@@ -48,12 +48,18 @@
 def kernel(
     n_space,
     n_wave,
-    noise_ref,
+    noise_hbm,
+    pos_hbm,
+    wave_hbm,
+    lists_hbm,
+    counts_hbm,
+    out_ref,
     pos_ref,
     wave_ref,
     lists_ref,
     counts_ref,
-    out_ref,
+    cacc,
+    back,
     ph_hi,
     ph_lo,
     posw,
@@ -61,7 +67,9 @@
     nf,
     bm_hi,
     bm_lo,
-    u,
+    u0,
+    u1_,
+    u2_,
     near,
     sbuf,
     rs,
@@ -85,12 +93,29 @@
     pos_r,
     norm_s,
     norm_r,
+    in_s,
 ):
     me = lax.axis_index("space")
     wv = lax.axis_index("wave")
     up = lax.rem(me + 1, n_space)
     down = lax.rem(me + n_space - 1, n_space)
     tiles = n_wave
+    u = (u0, u1_, u2_)
+
+    loads = [
+        pltpu.make_async_copy(pos_hbm, pos_ref, in_s.at[0]),
+        pltpu.make_async_copy(wave_hbm, wave_ref, in_s.at[1]),
+    ]
+    for t in range(tiles):
+        loads.append(
+            pltpu.make_async_copy(
+                noise_hbm.at[:, pl.ds(t * TILE, TILE)], u[0].at[tiles + t], in_s.at[4 + t]
+            )
+        )
+    loads.append(pltpu.make_async_copy(lists_hbm, lists_ref, in_s.at[2]))
+    loads.append(pltpu.make_async_copy(counts_hbm, counts_ref, in_s.at[3]))
+    for copy in loads:
+        copy.start()
 
     barrier = pltpu.get_barrier_semaphore()
 
@@ -119,12 +144,14 @@
             device_id_type=MESH,
         )
 
+    for copy in loads:
+        copy.wait()
+
     for t in range(tiles):
         lanes = slice(t * TILE, (t + 1) * TILE)
         posw[tiles + t] = jnp.concatenate(
             [pos_ref[:, lanes], jnp.zeros((5, TILE), F32)], axis=0
         )
-        u[0, tiles + t] = noise_ref[:, lanes]
 
     waves = wave_ref.shape[1]
     n_all = wave_ref[...].astype(F32)
@@ -167,13 +194,13 @@
                 ph_lo[rows, at : at + waves] = (value - high.astype(F32)).astype(BF16)
         return 0
 
-    lax.fori_loop(0, tiles, make_phases, 0)
+    lax.fori_loop(0, tiles // 2, make_phases, 0)
 
     def halo(k):
-        own = u.at[k, pl.ds(tiles, tiles)]
+        own = u[k].at[pl.ds(tiles, tiles)]
         return (
-            remote(own, u.at[k, pl.ds(0, tiles)], halo_s.at[k, 0], halo_r.at[k, 0], up, wv),
-            remote(own, u.at[k, pl.ds(2 * tiles, tiles)], halo_s.at[k, 1], halo_r.at[k, 1], down, wv),
+            remote(own, u[k].at[pl.ds(0, tiles)], halo_s.at[k, 0], halo_r.at[k, 0], up, wv),
+            remote(own, u[k].at[pl.ds(2 * tiles, tiles)], halo_s.at[k, 1], halo_r.at[k, 1], down, wv),
         )
 
     own_pos = posw.at[pl.ds(tiles, tiles)]
@@ -186,6 +213,8 @@
 
     for copy in pos_copies + halo(0):
         copy.start()
+
+    lax.fori_loop(tiles // 2, tiles, make_phases, 0)
 
     def pair_of(i):
         j = wv * (32 // n_wave) + i
@@ -238,7 +267,7 @@
 
         def one_pair(i, _):
             tile, source = pair_of(i)
-            f = u[k, source]
+            f = u[k][source]
             lhs = split_rows(jnp.concatenate([f[0:8], f[8:16], f[16:24]], axis=1))
             res = jnp.dot(lhs, bm_hi[i], preferred_element_type=F32) + jnp.dot(
                 lhs, bm_lo[i], preferred_element_type=F32
@@ -251,35 +280,64 @@
 
         lax.fori_loop(0, pairs, one_pair, 0)
 
+    my_y, my_x, my_c = lax.div(me, 8), lax.rem(lax.div(me, 2), 4), lax.rem(me, 2)
+    far = {0: 0, 1: 1, 2: 2, 3: 1}
+    steps = [(dy, dx, dc) for dy in range(4) for dx in range(4) for dc in range(2)]
+    steps = sorted(steps, key=lambda d: -(10 * (far[d[0]] + far[d[1]]) + d[2]))[:-1]
+    n_chips = n_space // 2
+    my_chip = lax.div(me, 2)
+    chip_steps = [(dy, dx) for dy in range(4) for dx in range(4)]
+    chip_steps = sorted(chip_steps, key=lambda d: -(far[d[0]] + far[d[1]]))
+
+    def chip_at(dy, dx):
+        return lax.rem(my_y + dy, 4) * 4 + lax.rem(my_x + dx, 4)
+
+    ring_order = [4, 3, 5, 2, 6, 1, 7]
+
     def send_space(src_of, dst, ssem, rsem):
-        def one(d, _):
-            peer = lax.rem(me + d, n_space)
+        for dy, dx, dc in steps:
+            peer = lax.rem(my_y + dy, 4) * 8 + lax.rem(my_x + dx, 4) * 2 + lax.rem(my_c + dc, 2)
             remote(src_of(peer), dst, ssem, rsem, peer, wv).start()
-            return 0
-
-        lax.fori_loop(1, n_space, one, 0)
+
+    def tile_at(d):
+        return lax.rem(wv + d, n_wave)
+
+    def phase_rows(ref, da, db, cols):
+        parts = []
+        for d in (da, db):
+            rows = pl.ds(pl.multiple_of(tile_at(d) * TILE, TILE), TILE)
+            parts.append(ref[rows, cols])
+        return jnp.concatenate(parts, axis=0)
 
     def all_but_one(ref, count, ssem, rsem):
         some = ref.at[pl.ds(0, count)]
         return remote(some, some, ssem, rsem, up, wv)
 
-    waiting = []
     sent = []
 
     for k in range(DEGREE):
-        x = jnp.concatenate([u[k, tiles + t] for t in range(tiles)], axis=1)
-        lhs = split_rows(x)
         step = 256
+        for first, (da, db) in enumerate(((0, 1), (7, 2), (6, 3), (5, 4))):
+            if k > 0:
+                for d in (da, db):
+                    if d > 0:
+                        piece = u[k].at[tiles + tile_at(d)]
+                        sem = n_wave - d
+                        remote(piece, piece, wa_s.at[k - 1], wa_r.at[k - 1, sem], up, wv).wait_recv()
+            x = jnp.concatenate([u[k][tiles + tile_at(da)], u[k][tiles + tile_at(db)]], axis=1)
+            lhs = split_rows(x)
+            for n in range(2 * waves // step):
+                cols = slice(n * step, (n + 1) * step)
+                c = jnp.dot(
+                    lhs, phase_rows(ph_hi, da, db, cols), preferred_element_type=F32
+                ) + jnp.dot(lhs, phase_rows(ph_lo, da, db, cols), preferred_element_type=F32)
+                if first == 0:
+                    cacc[:, cols] = c[0:24] + c[24:48]
+                else:
+                    cacc[:, cols] += c[0:24] + c[24:48]
         for n in range(waves // step):
-            parts = []
             for half in range(2):
-                cols = slice(half * waves + n * step, half * waves + (n + 1) * step)
-                c = jnp.dot(lhs, ph_hi[:, cols], preferred_element_type=F32) + jnp.dot(
-                    lhs, ph_lo[:, cols], preferred_element_type=F32
-                )
-                parts.append(c[0:24] + c[24:48])
-            for half in range(2):
-                c = parts[half]
+                c = cacc[:, half * waves + n * step : half * waves + (n + 1) * step]
                 for q in range(step // TILE):
                     lanes = slice(q * TILE, (q + 1) * TILE)
                     at = slice(n * step + q * TILE, n * step + (q + 1) * TILE)
@@ -288,17 +346,48 @@
                     d1 = ev[2, :, at] * c0 + ev[3, :, at] * c1 + ev[4, :, at] * c2
                     chip = half * (waves // TILE) + n * (step // TILE) + q
                     for tangent, d in ((0, d0), (1, d1)):
-                        slot = 2 * (tangent * (2 * waves // TILE) + chip)
-                        sbuf[k, slot] = d[0:4]
-                        sbuf[k, slot + 1] = d[4:8]
-        rs[k, me] = sbuf[k, me]
-        send_space(lambda peer: sbuf.at[k, peer], rs.at[k, me], rs_s.at[k], rs_r.at[k])
-        sent.append((sbuf.at[k], n_space - 1, rs_s.at[k], rs_r.at[k]))
+                        sbuf[k, tangent * (2 * waves // TILE) + chip] = d
+        for dy, dx in chip_steps:
+            peer = chip_at(dy, dx)
+
+            def send(peer=peer):
+                remote(
+                    sbuf.at[k, peer], rs.at[k, me], rs_s.at[k], rs_r.at[k], 2 * peer + 1, wv
+                ).start()
+
+            if (dy, dx) == (0, 0):
+                pl.when(my_c == 0)(send)
+            else:
+                send()
+
+        if k > 0:
+            for copy in halo(k):
+                copy.start()
+        if k == 0:
+            for copy in pos_copies:
+                copy.wait_recv()
+            lax.fori_loop(0, pairs, build_pair, 0)
+
+        @pl.when(my_c == 1)
+        def _():
+            all_but_one(rs.at[k], n_space - 1, rs_s.at[k], rs_r.at[k]).wait_recv()
+            rs[k, me] = sbuf[k, my_chip]
+            sums = [rs[k, s] + rs[k, s + 1] for s in range(0, n_space, 2)]
+            while len(sums) > 1:
+                sums = [sums[s] + sums[s + 1] for s in range(0, len(sums), 2)]
+            agb[k, my_chip] = sums[0]
+            for dy, dx in chip_steps:
+                for c in (0, 1):
+                    if (dy, dx, c) != (0, 0, 1):
+                        own = agb.at[k, my_chip]
+                        remote(
+                            own, own, ag_s.at[k], ag_r.at[k], 2 * chip_at(dy, dx) + c, wv
+                        ).start()
 
         if k > 0:
             total = jnp.zeros((8, TILE), F32)
             for t in range(tiles):
-                v = u[k, tiles + t]
+                v = u[k][tiles + t]
                 v = v * v
                 total = total + (v[0:8] + v[8:16] + v[16:24])
             lane_sum = jnp.sum(total, axis=1, keepdims=True)
@@ -316,22 +405,18 @@
             )
             sent.append((nrecv.at[k - 1], n_space - 1, norm_s.at[k - 1], norm_r.at[k - 1]))
 
-        if k == 0:
-            for copy in pos_copies:
-                copy.wait_recv()
-            lax.fori_loop(0, pairs, build_pair, 0)
         for copy in halo(k):
             copy.wait_recv()
         near_apply(k)
 
-        all_but_one(rs.at[k], n_space - 1, rs_s.at[k], rs_r.at[k]).wait_recv()
-        total = rs[k, 0]
-        for s in range(1, n_space):
-            total = total + rs[k, s]
-        agb[k, me] = total
-        send_space(lambda peer: agb.at[k, me], agb.at[k, me], ag_s.at[k], ag_r.at[k])
-        sent.append((agb.at[k], n_space - 1, ag_s.at[k], ag_r.at[k]))
-        all_but_one(agb.at[k], n_space - 1, ag_s.at[k], ag_r.at[k]).wait_recv()
+        @pl.when(my_c == 0)
+        def _():
+            all_but_one(agb.at[k], n_chips, ag_s.at[k], ag_r.at[k]).wait_recv()
+
+        @pl.when(my_c == 1)
+        def _():
+            all_but_one(agb.at[k], n_chips - 1, ag_s.at[k], ag_r.at[k]).wait_recv()
+
 
         rows = [[], [], []]
         for half in range(2):
@@ -340,8 +425,7 @@
                 chip = half * (waves // TILE) + n
                 d = []
                 for tangent in range(2):
-                    slot = 2 * (tangent * (2 * waves // TILE) + chip)
-                    d.append(jnp.concatenate([agb[k, slot], agb[k, slot + 1]], axis=0))
+                    d.append(agb[k, tangent * (2 * waves // TILE) + chip])
                 rows[0].append(ev[0, :, at] * d[0] + ev[2, :, at] * d[1])
                 rows[1].append(ev[1, :, at] * d[0] + ev[3, :, at] * d[1])
                 rows[2].append(ev[4, :, at] * d[1])
@@ -349,24 +433,38 @@
             jnp.concatenate([jnp.concatenate(r, axis=1) for r in rows], axis=0)
         )
         contract = (((1,), (1,)), ((), ()))
-        for n in range(tiles // 2):
-            span = slice(n * 2 * TILE, (n + 1) * 2 * TILE)
+        every = slice(0, 2 * waves)
+        back[...] = lhs
+
+        def back_pair(i, _):
+            da, db = n_wave // 2 + i, n_wave // 2 - 1 - i
             v = lax.dot_general(
-                lhs, ph_hi[span, :], contract, preferred_element_type=F32
-            ) + lax.dot_general(lhs, ph_lo[span, :], contract, preferred_element_type=F32)
+                back[...], phase_rows(ph_hi, da, db, every), contract, preferred_element_type=F32
+            ) + lax.dot_general(
+                back[...], phase_rows(ph_lo, da, db, every), contract, preferred_element_type=F32
+            )
             v = v[0:24] + v[24:48]
-            for q in range(2):
-                t = 2 * n + q
+
+            def part(d, q):
+                t = tile_at(d)
                 vbuf[k, t] = v[:, q * TILE : (q + 1) * TILE] + near[t]
-
-        wr[k, wv] = vbuf[k, wv] + u[k, tiles + wv]
-
-        def send_part(d, _):
-            peer = lax.rem(wv + d, n_wave)
-            remote(vbuf.at[k, peer], wr.at[k, wv], wr_s.at[k], wr_r.at[k], me, peer).start()
+                return t
+
+            def send(t):
+                remote(vbuf.at[k, t], wr.at[k, wv], wr_s.at[k], wr_r.at[k], me, t).start()
+
+            t = part(da, 0)
+            send(t)
+            t = part(db, 1)
+
+            @pl.when(db > 0)
+            def _():
+                send(t)
+
             return 0
 
-        lax.fori_loop(1, n_wave, send_part, 0)
+        lax.fori_loop(0, n_wave // 2, back_pair, 0)
+        wr[k, wv] = vbuf[k, wv] + u[k][tiles + wv]
         sent.append((wr.at[k], n_wave - 1, wr_s.at[k], wr_r.at[k]))
         all_but_one(wr.at[k], n_wave - 1, wr_s.at[k], wr_r.at[k]).wait_recv()
         image = wr[k, 0]
@@ -374,9 +472,9 @@
             image = image + wr[k, w]
 
         if k < DEGREE - 1:
-            own = u.at[k + 1, tiles + wv]
-            u[k + 1, tiles + wv] = image
-            whole = u.at[k + 1, pl.ds(tiles, tiles)]
+            own = u[k + 1].at[tiles + wv]
+            u[k + 1][tiles + wv] = image
+            whole = u[k + 1].at[pl.ds(tiles, tiles)]
         else:
             for j in range(2):
                 all_but_one(nrecv.at[j], n_space - 1, norm_s.at[j], norm_r.at[j]).wait_recv()
@@ -405,9 +503,9 @@
             pieces = []
             for c in range(3):
                 at = slice(c * 8, (c + 1) * 8)
-                f = u[0, tiles + wv, at]
-                u1 = u[1, tiles + wv, at]
-                u2 = u[2, tiles + wv, at]
+                f = u[0][tiles + wv, at]
+                u1 = u[1][tiles + wv, at]
+                u2 = u[2][tiles + wv, at]
                 u3 = image[at]
                 t1 = (2.0 * u1 - bound_sum * f) * scale
                 mt1 = (2.0 * u2 - bound_sum * u1) * scale
@@ -420,18 +518,26 @@
             outb[wv] = jnp.concatenate(pieces, axis=0)
             whole = outb
 
-        def send_tile(d, _):
-            remote(own, own, wa_s.at[k], wa_r.at[k], me, lax.rem(wv + d, n_wave)).start()
-            return 0
-
-        lax.fori_loop(1, n_wave, send_tile, 0)
-        sent.append((whole, n_wave - 1, wa_s.at[k], wa_r.at[k]))
-        all_but_one(whole, n_wave - 1, wa_s.at[k], wa_r.at[k]).wait_recv()
-        if k < DEGREE - 1:
-            for copy in halo(k + 1):
-                copy.start()
-
-    out_ref[...] = outb[...]
+        for d in ring_order:
+            remote(own, own, wa_s.at[k], wa_r.at[k, d], me, tile_at(d)).start()
+        sent.append((whole, n_wave - 1, wa_s.at[k], wa_r.at[k, 0]))
+
+    out_ref[wv] = outb[wv]
+    for d in (1, 7, 2, 6, 3, 5, 4):
+        piece = outb.at[tile_at(d)]
+        remote(piece, piece, wa_s.at[2], wa_r.at[2, n_wave - d], up, wv).wait_recv()
+        out_ref[tile_at(d)] = outb[tile_at(d)]
+    for k in range(DEGREE):
+
+        @pl.when(my_c == 0)
+        def _():
+            all_but_one(sbuf.at[k], n_chips, rs_s.at[k], rs_r.at[k]).wait_send()
+
+        @pl.when(my_c == 1)
+        def _():
+            all_but_one(sbuf.at[k], n_chips - 1, rs_s.at[k], rs_r.at[k]).wait_send()
+            all_but_one(rs.at[k], n_space - 1, ag_s.at[k], ag_r.at[k]).wait_send()
+
     for ref, count, ssem, rsem in sent:
         all_but_one(ref, count, ssem, rsem).wait_send()
     for copy in pos_copies:
@@ -450,15 +556,21 @@
     arranged = jnp.transpose(noise, (1, 0, 2)).reshape(rows, count)
     pairs = 32 // n_wave
     vmem = pl.BlockSpec(memory_space=pltpu.VMEM)
-    smem = pl.BlockSpec(memory_space=pltpu.SMEM)
     dma = pltpu.SemaphoreType.DMA
 
+    hbm = pl.BlockSpec(memory_space=pl.ANY)
     out = pl.pallas_call(
         functools.partial(kernel, n_space, n_wave),
         out_shape=jax.ShapeDtypeStruct((tiles, rows, TILE), F32),
-        in_specs=[vmem, vmem, vmem, smem, smem],
+        in_specs=[hbm] * 5,
         out_specs=vmem,
         scratch_shapes=[
+            pltpu.VMEM((3, count), F32),
+            pltpu.VMEM((3, waves), jnp.int32),
+            pltpu.SMEM(tile_lists.shape, jnp.int32),
+            pltpu.SMEM(tile_counts.shape, jnp.int32),
+            pltpu.VMEM((rows, 2 * waves), F32),
+            pltpu.VMEM((2 * rows, 2 * waves), BF16),
             pltpu.VMEM((count, 2 * waves), BF16),
             pltpu.VMEM((count, 2 * waves), BF16),
             pltpu.VMEM((3 * tiles, 8, TILE), F32),
@@ -466,11 +578,13 @@
             pltpu.VMEM((3, 8, waves), F32),
             pltpu.VMEM((pairs, 3 * TILE, 3 * TILE), BF16),
             pltpu.VMEM((pairs, 3 * TILE, 3 * TILE), BF16),
-            pltpu.VMEM((DEGREE, 3 * tiles, rows, TILE), F32),
+            pltpu.VMEM((3 * tiles, rows, TILE), F32),
+            pltpu.VMEM((3 * tiles, rows, TILE), F32),
+            pltpu.VMEM((3 * tiles, rows, TILE), F32),
             pltpu.VMEM((tiles, rows, TILE), F32),
-            pltpu.VMEM((DEGREE, n_space, 4, TILE), F32),
-            pltpu.VMEM((DEGREE, n_space, 4, TILE), F32),
-            pltpu.VMEM((DEGREE, n_space, 4, TILE), F32),
+            pltpu.VMEM((DEGREE, n_space // 2, 8, TILE), F32),
+            pltpu.VMEM((DEGREE, n_space, 8, TILE), F32),
+            pltpu.VMEM((DEGREE, n_space // 2, 8, TILE), F32),
             pltpu.VMEM((DEGREE, tiles, rows, TILE), F32),
             pltpu.VMEM((DEGREE, tiles, rows, TILE), F32),
             pltpu.VMEM((2, 1, TILE), F32),
@@ -483,16 +597,17 @@
             dma((DEGREE,)),
             dma((DEGREE,)),
             dma((DEGREE,)),
-            dma((DEGREE,)),
+            dma((DEGREE, n_wave)),
             dma((DEGREE, 2)),
             dma((DEGREE, 2)),
             dma((2,)),
             dma((2,)),
             dma((2,)),
             dma((2,)),
+            dma((4 + tiles,)),
         ],
         compiler_params=pltpu.CompilerParams(
-            collective_id=0, has_side_effects=True, vmem_limit_bytes=32 * 1024 * 1024
+            collective_id=0, has_side_effects=True, vmem_limit_bytes=60 * 1024 * 1024
         ),
     )(arranged, positions, wave_index, tile_lists, tile_counts)
     out = out.reshape(tiles, 3, vectors, TILE)

time: 84.2 us -> 73.4 us (0.87)
  Pallas kernels: 79.7 us -> 71.5 us
  local copies, waits for them, and re-layouts: 4.29 us -> 1.54 us
    pallas_call x1, Pallas kernels: 79.7 us -> 71.5 us  [body(): pl.pallas_call(functools.partial(kernel, n_space, n_wave), out_shape=jax....]
    unnamed x10 -> x0, local copies, waits for them, and re-layouts: 3.65 us -> none
    reshape x1, local copies, waits for them, and re-layouts: 0.65 us -> 1.54 us  [body(): return jnp.transpose(out, (2, 1, 0, 3)).reshape(vectors, 3, count)]
where the time goes in v2:
time: 73.4 us; the launch traced here: 73.1 us
  Pallas kernels  71.5 us (97%)
  local copies, waits for them, and re-layouts  1.54 us (2%)
    pallas_call x1, Pallas kernels, body(): pl.pallas_call(functools.partial(kernel, n_space, n_wave), out_shape=jax....  71.5 us
    reshape x1, local copies, waits for them, and re-layouts, body(): return jnp.transpose(out, (2, 1, 0, 3)).reshape(vectors, 3, count)  1.54 us

profile of v2, /device:TPU:1, one launch (start us, length us, event | category | flops | bytes accessed | tf_op | source)
XLA Modules:
  0.0 73.1 jit_solution(9925635558076971371)
XLA Ops:
  0.0 71.5 %shard_map.55 = f32[8,24,128]{2,1,0:T(8,128)} custom-call(f32[24,1024]{1,0:T(8,128)} %bitcast.10, f32[3,1024]{1,0:T(4,128)} %pos_hbm.1, s32[3,512]{1,0:T(4,128)} %wave_hbm.1, s32[8,8]{1,0:T(8,128)} %lists_hbm.1, s32[8]{0:T(128)} %counts_hbm.1), custom_call_target="tpu_custom_call" | custom-call | tf_op jit(solution)/shard_map/pallas_call | solution.py:562
  71.5 1.5 %copy_bitcast_fusion = f32[8,3,1024]{2,0,1:T(8,128)} fusion(f32[8,24,128]{2,1,0:T(8,128)} %shard_map.55), kind=kLoop, calls=%fused_computation | loop fusion | bytes 196608 | tf_op jit(solution)/shard_map/reshape | solution.py:614

commit v3 on v2

--- a/solution.py
+++ b/solution.py
@@ -25,7 +25,8 @@
 SPREAD = 100.0
 EPSILON = 1e-06
 
-SINE = (6.283185160087367, -41.34165503087954, 81.60100403735636, -76.54978142115317, 39.5366991046531)
+ODD = (-6.283185160088051, 41.34165503105119, -81.60100404875506, 76.54978169659269, -39.53670129282338)
+EVEN = (0.9999999534612963, -19.739171433341692, 64.93459053611144, -85.24032812693831, 56.242362994696336)
 
 
 def split_rows(x):
@@ -33,16 +34,11 @@
     return jnp.concatenate([high, x - high], axis=0).astype(BF16)
 
 
-def sine_of_turns(a):
-    a2 = a * a
-    p = F32(SINE[-1])
-    for c in SINE[-2::-1]:
-        p = p * a2 + F32(c)
-    return p * a
-
-
-def nearest(x):
-    return jnp.floor(x + 0.5)
+def polynomial(coeffs, x):
+    p = F32(coeffs[-1])
+    for c in coeffs[-2::-1]:
+        p = p * x + F32(c)
+    return p
 
 
 def kernel(
@@ -62,9 +58,15 @@
     back,
     ph_hi,
     ph_lo,
+    pt_hi,
+    pt_lo,
     posw,
     ev,
     nf,
+    nt,
+    pf,
+    turns,
+    turns_t,
     bm_hi,
     bm_lo,
     u0,
@@ -144,7 +146,7 @@
             device_id_type=MESH,
         )
 
-    for copy in loads:
+    for copy in loads[:2]:
         copy.wait()
 
     for t in range(tiles):
@@ -171,30 +173,80 @@
     ev[2] = -root * ka * kc / (rho * length)
     ev[3] = -root * kb * kc / (rho * length)
     ev[4] = root * rho / length
-    for c in range(3):
-        nf[c] = n_rows[c]
-
-    def make_phases(t, _):
-        cols = jnp.transpose(posw[tiles + t])
+    padded = jnp.concatenate([n_all, jnp.zeros((5, waves), F32)], axis=0)
+    padded = jnp.concatenate([padded] * 3, axis=0)
+    nf[...] = padded.astype(BF16)
+    for n in range(waves // TILE):
+        at = slice(n * TILE, (n + 1) * TILE)
+        nt[at, :] = jnp.transpose(padded[:, at]).astype(BF16)
+    sides = jnp.where(
+        lax.broadcasted_iota(jnp.int32, (8, TILE), 0) == 0, F32(1.0 / n_space), F32(1.0 / SIDE_CROSS)
+    )
+
+    def trig(angle):
+        r = angle - jnp.floor(angle + 0.5)
+        b = jnp.abs(r) - 0.25
+        b2 = b * b
+        cosine = polynomial(ODD, b2) * b
+        sine = polynomial(EVEN, b2)
+        sine = jnp.where(r < 0.0, -sine, sine)
+        halves = []
+        for value in (cosine, sine):
+            high = value.astype(BF16)
+            halves.append((high, (value - high.astype(F32)).astype(BF16)))
+        return halves
+
+    def make_phases(t):
+        box = posw[tiles + t] * sides
+        first = box.astype(BF16).astype(F32)
+        second = (box - first).astype(BF16).astype(F32)
+        pieces = jnp.concatenate([first, second, box - first - second], axis=0)
+        pf[:, pl.ds(pl.multiple_of(t * TILE, TILE), TILE)] = pieces.astype(BF16)
+        turns[...] = jnp.dot(
+            jnp.transpose(pieces).astype(BF16), nf[...], preferred_element_type=F32
+        )
         for j in range(TILE // 16):
             rows = pl.ds(pl.multiple_of(t * TILE + j * 16, 16), 16)
-            part = cols[j * 16 : (j + 1) * 16]
-            tx = part[:, 0:1] * F32(1.0 / n_space)
-            ty = part[:, 1:2] * F32(1.0 / SIDE_CROSS)
-            tz = part[:, 2:3] * F32(1.0 / SIDE_CROSS)
-            turns = tx * nf[0, 0:1] + ty * nf[1, 0:1] + tz * nf[2, 0:1]
-            r = turns - nearest(turns)
-            q = r - 0.25
-            q = q - nearest(q)
-            cosine = sine_of_turns(0.25 - jnp.abs(r))
-            sine = sine_of_turns(0.25 - jnp.abs(q))
-            for at, value in ((0, cosine), (waves, sine)):
-                high = value.astype(BF16)
+            for at, (high, low) in zip((0, waves), trig(turns[j * 16 : (j + 1) * 16])):
                 ph_hi[rows, at : at + waves] = high
-                ph_lo[rows, at : at + waves] = (value - high.astype(F32)).astype(BF16)
+                ph_lo[rows, at : at + waves] = low
+
+    def make_transposed(n, _):
+        block = nt[pl.ds(pl.multiple_of(n * TILE, TILE), TILE), :]
+        turns_t[...] = jnp.dot(block, pf[...], preferred_element_type=F32)
+        for j in range(TILE // 16):
+            for half in range(2):
+                lanes = slice(half * waves, (half + 1) * waves)
+                parts = trig(turns_t[j * 16 : (j + 1) * 16, lanes])
+                for at, (high, low) in zip((0, waves), parts):
+                    rows = pl.ds(pl.multiple_of(at + n * TILE + j * 16, 16), 16)
+                    pt_hi[rows, lanes] = high
+                    pt_lo[rows, lanes] = low
         return 0
 
-    lax.fori_loop(0, tiles // 2, make_phases, 0)
+    step = 256
+
+    def fold(t):
+        lhs = split_rows(u[0][tiles + t])
+        rows = pl.ds(pl.multiple_of(t * TILE, TILE), TILE)
+        for n in range(2 * waves // step):
+            cols = slice(n * step, (n + 1) * step)
+            c = jnp.dot(lhs, ph_hi[rows, cols], preferred_element_type=F32) + jnp.dot(
+                lhs, ph_lo[rows, cols], preferred_element_type=F32
+            )
+            cacc[:, cols] += c[0:24] + c[24:48]
+
+    def fold_and_make(t, _):
+        fold(t - 1)
+        make_phases(t)
+        return 0
+
+    cacc[...] = jnp.zeros_like(cacc)
+    make_phases(0)
+    for copy in loads[2:]:
+        copy.wait()
+    lax.fori_loop(1, tiles, fold_and_make, 0)
+    fold(tiles - 1)
 
     def halo(k):
         own = u[k].at[pl.ds(tiles, tiles)]
@@ -208,13 +260,6 @@
         remote(own_pos, posw.at[pl.ds(0, tiles)], pos_s.at[0], pos_r.at[0], up, wv),
         remote(own_pos, posw.at[pl.ds(2 * tiles, tiles)], pos_s.at[1], pos_r.at[1], down, wv),
     )
-
-    pl.semaphore_wait(barrier, n_space - 1 + n_wave - 1)
-
-    for copy in pos_copies + halo(0):
-        copy.start()
-
-    lax.fori_loop(tiles // 2, tiles, make_phases, 0)
 
     def pair_of(i):
         j = wv * (32 // n_wave) + i
@@ -302,6 +347,13 @@
     def tile_at(d):
         return lax.rem(wv + d, n_wave)
 
+    def phase_cols(ref, da, db):
+        parts = []
+        for d in (da, db):
+            cols = pl.ds(pl.multiple_of(tile_at(d) * TILE, TILE), TILE)
+            parts.append(ref[:, cols])
+        return jnp.concatenate(parts, axis=1)
+
     def phase_rows(ref, da, db, cols):
         parts = []
         for d in (da, db):
@@ -316,14 +368,12 @@
     sent = []
 
     for k in range(DEGREE):
-        step = 256
-        for first, (da, db) in enumerate(((0, 1), (7, 2), (6, 3), (5, 4))):
-            if k > 0:
-                for d in (da, db):
-                    if d > 0:
-                        piece = u[k].at[tiles + tile_at(d)]
-                        sem = n_wave - d
-                        remote(piece, piece, wa_s.at[k - 1], wa_r.at[k - 1, sem], up, wv).wait_recv()
+        for first, (da, db) in enumerate(((0, 1), (7, 2), (6, 3), (5, 4)) if k > 0 else ()):
+            for d in (da, db):
+                if d > 0:
+                    piece = u[k].at[tiles + tile_at(d)]
+                    sem = n_wave - d
+                    remote(piece, piece, wa_s.at[k - 1], wa_r.at[k - 1, sem], up, wv).wait_recv()
             x = jnp.concatenate([u[k][tiles + tile_at(da)], u[k][tiles + tile_at(db)]], axis=1)
             lhs = split_rows(x)
             for n in range(2 * waves // step):
@@ -347,6 +397,8 @@
                     chip = half * (waves // TILE) + n * (step // TILE) + q
                     for tangent, d in ((0, d0), (1, d1)):
                         sbuf[k, tangent * (2 * waves // TILE) + chip] = d
+        if k == 0:
+            pl.semaphore_wait(barrier, n_space - 1 + n_wave - 1)
         for dy, dx in chip_steps:
             peer = chip_at(dy, dx)
 
@@ -360,13 +412,10 @@
             else:
                 send()
 
-        if k > 0:
-            for copy in halo(k):
-                copy.start()
+        for copy in (pos_copies if k == 0 else ()) + halo(k):
+            copy.start()
         if k == 0:
-            for copy in pos_copies:
-                copy.wait_recv()
-            lax.fori_loop(0, pairs, build_pair, 0)
+            lax.fori_loop(0, waves // TILE, make_transposed, 0)
 
         @pl.when(my_c == 1)
         def _():
@@ -405,6 +454,10 @@
             )
             sent.append((nrecv.at[k - 1], n_space - 1, norm_s.at[k - 1], norm_r.at[k - 1]))
 
+        if k == 0:
+            for copy in pos_copies:
+                copy.wait_recv()
+            lax.fori_loop(0, pairs, build_pair, 0)
         for copy in halo(k):
             copy.wait_recv()
         near_apply(k)
@@ -432,16 +485,12 @@
         lhs = split_rows(
             jnp.concatenate([jnp.concatenate(r, axis=1) for r in rows], axis=0)
         )
-        contract = (((1,), (1,)), ((), ()))
-        every = slice(0, 2 * waves)
         back[...] = lhs
 
         def back_pair(i, _):
             da, db = n_wave // 2 + i, n_wave // 2 - 1 - i
-            v = lax.dot_general(
-                back[...], phase_rows(ph_hi, da, db, every), contract, preferred_element_type=F32
-            ) + lax.dot_general(
-                back[...], phase_rows(ph_lo, da, db, every), contract, preferred_element_type=F32
+            v = jnp.dot(back[...], phase_cols(pt_hi, da, db), preferred_element_type=F32) + jnp.dot(
+                back[...], phase_cols(pt_lo, da, db), preferred_element_type=F32
             )
             v = v[0:24] + v[24:48]
 
@@ -573,9 +622,15 @@
             pltpu.VMEM((2 * rows, 2 * waves), BF16),
             pltpu.VMEM((count, 2 * waves), BF16),
             pltpu.VMEM((count, 2 * waves), BF16),
+            pltpu.VMEM((2 * waves, count), BF16),
+            pltpu.VMEM((2 * waves, count), BF16),
             pltpu.VMEM((3 * tiles, 8, TILE), F32),
             pltpu.VMEM((5, 8, waves), F32),
-            pltpu.VMEM((3, 8, waves), F32),
+            pltpu.VMEM((24, waves), BF16),
+            pltpu.VMEM((waves, 24), BF16),
+            pltpu.VMEM((24, count), BF16),
+            pltpu.VMEM((TILE, waves), F32),
+            pltpu.VMEM((TILE, count), F32),
             pltpu.VMEM((pairs, 3 * TILE, 3 * TILE), BF16),
             pltpu.VMEM((pairs, 3 * TILE, 3 * TILE), BF16),
             pltpu.VMEM((3 * tiles, rows, TILE), F32),

time: 73.4 us -> 72.3 us (0.985)
  Pallas kernels: 71.5 us -> 70.6 us
    pallas_call x1, Pallas kernels: 71.5 us -> 70.6 us  [body(): pl.pallas_call(functools.partial(kernel, n_space, n_wave), out_shape=jax....]
where the time goes in v3:
time: 72.3 us; the launch traced here: 72.1 us
  Pallas kernels  70.6 us (98%)
  local copies, waits for them, and re-layouts  1.54 us (2%)
    pallas_call x1, Pallas kernels, body(): pl.pallas_call(functools.partial(kernel, n_space, n_wave), out_shape=jax....  70.6 us
    reshape x1, local copies, waits for them, and re-layouts, body(): return jnp.transpose(out, (2, 1, 0, 3)).reshape(vectors, 3, count)  1.54 us

profile of v3, /device:TPU:1, one launch (start us, length us, event | category | flops | bytes accessed | tf_op | source)
XLA Modules:
  0.0 72.1 jit_solution(12232743079907330080)
XLA Ops:
  0.0 70.6 %shard_map.55 = f32[8,24,128]{2,1,0:T(8,128)} custom-call(f32[24,1024]{1,0:T(8,128)} %bitcast.10, f32[3,1024]{1,0:T(4,128)} %pos_hbm.1, s32[3,512]{1,0:T(4,128)} %wave_hbm.1, s32[8,8]{1,0:T(8,128)} %lists_hbm.1, s32[8]{0:T(128)} %counts_hbm.1), custom_call_target="tpu_custom_call" | custom-call | tf_op jit(solution)/shard_map/pallas_call | solution.py:611
  70.6 1.5 %copy_bitcast_fusion = f32[8,3,1024]{2,0,1:T(8,128)} fusion(f32[8,24,128]{2,1,0:T(8,128)} %shard_map.55), kind=kLoop, calls=%fused_computation | loop fusion | bytes 196608 | tf_op jit(solution)/shard_map/reshape | solution.py:669

commit v4 on v3

--- a/solution.py
+++ b/solution.py
@@ -25,13 +25,17 @@
 SPREAD = 100.0
 EPSILON = 1e-06
 
-ODD = (-6.283185160088051, 41.34165503105119, -81.60100404875506, 76.54978169659269, -39.53670129282338)
-EVEN = (0.9999999534612963, -19.739171433341692, 64.93459053611144, -85.24032812693831, 56.242362994696336)
+ODD = (4.442882834148948, -7.308241154482914, 3.6062889571583123, -0.8457635896353835, 0.10920574060672703)
+EVEN = (1.4142134965574307, -6.978850987759868, 5.7394611627073875, -1.8835629390376682, 0.31069809581455876)
 
 
 def split_rows(x):
     high = x.astype(BF16).astype(F32)
     return jnp.concatenate([high, x - high], axis=0).astype(BF16)
+
+
+def nearest(x):
+    return lax.round(x, lax.RoundingMethod.TO_NEAREST_EVEN)
 
 
 def polynomial(coeffs, x):
@@ -184,20 +188,28 @@
     )
 
     def trig(angle):
-        r = angle - jnp.floor(angle + 0.5)
-        b = jnp.abs(r) - 0.25
-        b2 = b * b
-        cosine = polynomial(ODD, b2) * b
-        sine = polynomial(EVEN, b2)
-        sine = jnp.where(r < 0.0, -sine, sine)
+        r = angle - nearest(angle)
+        r2 = r * r
+        half_sine = polynomial(ODD, r2) * r
+        cosine = 1.0 - half_sine * half_sine
+        sine = half_sine * polynomial(EVEN, r2)
         halves = []
         for value in (cosine, sine):
             high = value.astype(BF16)
             halves.append((high, (value - high.astype(F32)).astype(BF16)))
         return halves
 
+    def tile_at(d):
+        return lax.rem(wv + d, n_wave)
+
+    def distance(j):
+        if isinstance(j, int):
+            return (j + 1) // 2 if j % 2 == 1 else (n_wave - j // 2) % n_wave
+        half = lax.div(j + 1, 2)
+        return jnp.where(lax.rem(j, 2) == 1, half, lax.rem(n_wave - half, n_wave))
+
     def make_phases(t):
-        box = posw[tiles + t] * sides
+        box = posw[tiles + tile_at(distance(t))] * sides
         first = box.astype(BF16).astype(F32)
         second = (box - first).astype(BF16).astype(F32)
         pieces = jnp.concatenate([first, second, box - first - second], axis=0)
@@ -215,19 +227,19 @@
         block = nt[pl.ds(pl.multiple_of(n * TILE, TILE), TILE), :]
         turns_t[...] = jnp.dot(block, pf[...], preferred_element_type=F32)
         for j in range(TILE // 16):
-            for half in range(2):
-                lanes = slice(half * waves, (half + 1) * waves)
+            for pair in range(tiles // 2):
+                lanes = slice(pair * 2 * TILE, (pair + 1) * 2 * TILE)
                 parts = trig(turns_t[j * 16 : (j + 1) * 16, lanes])
                 for at, (high, low) in zip((0, waves), parts):
                     rows = pl.ds(pl.multiple_of(at + n * TILE + j * 16, 16), 16)
-                    pt_hi[rows, lanes] = high
-                    pt_lo[rows, lanes] = low
+                    pt_hi[pair, rows, :] = high
+                    pt_lo[pair, rows, :] = low
         return 0
 
     step = 256
 
     def fold(t):
-        lhs = split_rows(u[0][tiles + t])
+        lhs = split_rows(u[0][tiles + tile_at(distance(t))])
         rows = pl.ds(pl.multiple_of(t * TILE, TILE), TILE)
         for n in range(2 * waves // step):
             cols = slice(n * step, (n + 1) * step)
@@ -344,23 +356,6 @@
             peer = lax.rem(my_y + dy, 4) * 8 + lax.rem(my_x + dx, 4) * 2 + lax.rem(my_c + dc, 2)
             remote(src_of(peer), dst, ssem, rsem, peer, wv).start()
 
-    def tile_at(d):
-        return lax.rem(wv + d, n_wave)
-
-    def phase_cols(ref, da, db):
-        parts = []
-        for d in (da, db):
-            cols = pl.ds(pl.multiple_of(tile_at(d) * TILE, TILE), TILE)
-            parts.append(ref[:, cols])
-        return jnp.concatenate(parts, axis=1)
-
-    def phase_rows(ref, da, db, cols):
-        parts = []
-        for d in (da, db):
-            rows = pl.ds(pl.multiple_of(tile_at(d) * TILE, TILE), TILE)
-            parts.append(ref[rows, cols])
-        return jnp.concatenate(parts, axis=0)
-
     def all_but_one(ref, count, ssem, rsem):
         some = ref.at[pl.ds(0, count)]
         return remote(some, some, ssem, rsem, up, wv)
@@ -368,20 +363,23 @@
     sent = []
 
     for k in range(DEGREE):
-        for first, (da, db) in enumerate(((0, 1), (7, 2), (6, 3), (5, 4)) if k > 0 else ()):
-            for d in (da, db):
+        groups = ((0, 1), (2, 3), (4, 5), (6,), (7,)) if k > 0 else ()
+        for group in groups:
+            for j in group:
+                d = distance(j)
                 if d > 0:
                     piece = u[k].at[tiles + tile_at(d)]
                     sem = n_wave - d
                     remote(piece, piece, wa_s.at[k - 1], wa_r.at[k - 1, sem], up, wv).wait_recv()
-            x = jnp.concatenate([u[k][tiles + tile_at(da)], u[k][tiles + tile_at(db)]], axis=1)
-            lhs = split_rows(x)
+            x = [u[k][tiles + tile_at(distance(j))] for j in group]
+            lhs = split_rows(jnp.concatenate(x, axis=1))
+            rows = slice(group[0] * TILE, (group[-1] + 1) * TILE)
             for n in range(2 * waves // step):
                 cols = slice(n * step, (n + 1) * step)
-                c = jnp.dot(
-                    lhs, phase_rows(ph_hi, da, db, cols), preferred_element_type=F32
-                ) + jnp.dot(lhs, phase_rows(ph_lo, da, db, cols), preferred_element_type=F32)
-                if first == 0:
+                c = jnp.dot(lhs, ph_hi[rows, cols], preferred_element_type=F32) + jnp.dot(
+                    lhs, ph_lo[rows, cols], preferred_element_type=F32
+                )
+                if group[0] == 0:
                     cacc[:, cols] = c[0:24] + c[24:48]
                 else:
                     cacc[:, cols] += c[0:24] + c[24:48]
@@ -488,9 +486,9 @@
         back[...] = lhs
 
         def back_pair(i, _):
-            da, db = n_wave // 2 + i, n_wave // 2 - 1 - i
-            v = jnp.dot(back[...], phase_cols(pt_hi, da, db), preferred_element_type=F32) + jnp.dot(
-                back[...], phase_cols(pt_lo, da, db), preferred_element_type=F32
+            pair = tiles // 2 - 1 - i
+            v = jnp.dot(back[...], pt_hi[pair], preferred_element_type=F32) + jnp.dot(
+                back[...], pt_lo[pair], preferred_element_type=F32
             )
             v = v[0:24] + v[24:48]
 
@@ -502,11 +500,10 @@
             def send(t):
                 remote(vbuf.at[k, t], wr.at[k, wv], wr_s.at[k], wr_r.at[k], me, t).start()
 
-            t = part(da, 0)
-            send(t)
-            t = part(db, 1)
-
-            @pl.when(db > 0)
+            send(part(distance(2 * pair + 1), 1))
+            t = part(distance(2 * pair), 0)
+
+            @pl.when(pair > 0)
             def _():
                 send(t)
 
@@ -515,16 +512,7 @@
         lax.fori_loop(0, n_wave // 2, back_pair, 0)
         wr[k, wv] = vbuf[k, wv] + u[k][tiles + wv]
         sent.append((wr.at[k], n_wave - 1, wr_s.at[k], wr_r.at[k]))
-        all_but_one(wr.at[k], n_wave - 1, wr_s.at[k], wr_r.at[k]).wait_recv()
-        image = wr[k, 0]
-        for w in range(1, n_wave):
-            image = image + wr[k, w]
-
-        if k < DEGREE - 1:
-            own = u[k + 1].at[tiles + wv]
-            u[k + 1][tiles + wv] = image
-            whole = u[k + 1].at[pl.ds(tiles, tiles)]
-        else:
+        if k == DEGREE - 1:
             for j in range(2):
                 all_but_one(nrecv.at[j], n_space - 1, norm_s.at[j], norm_r.at[j]).wait_recv()
             sums = []
@@ -549,6 +537,16 @@
                 coeffs.append(c * F32((1.0 if order == 0 else 2.0) / nodes))
             bound_sum = high + low
             scale = 1.0 / (high - low)
+        all_but_one(wr.at[k], n_wave - 1, wr_s.at[k], wr_r.at[k]).wait_recv()
+        image = wr[k, 0]
+        for w in range(1, n_wave):
+            image = image + wr[k, w]
+
+        if k < DEGREE - 1:
+            own = u[k + 1].at[tiles + wv]
+            u[k + 1][tiles + wv] = image
+            whole = u[k + 1].at[pl.ds(tiles, tiles)]
+        else:
             pieces = []
             for c in range(3):
                 at = slice(c * 8, (c + 1) * 8)
@@ -622,8 +620,8 @@
             pltpu.VMEM((2 * rows, 2 * waves), BF16),
             pltpu.VMEM((count, 2 * waves), BF16),
             pltpu.VMEM((count, 2 * waves), BF16),
-            pltpu.VMEM((2 * waves, count), BF16),
-            pltpu.VMEM((2 * waves, count), BF16),
+            pltpu.VMEM((tiles // 2, 2 * waves, 2 * TILE), BF16),
+            pltpu.VMEM((tiles // 2, 2 * waves, 2 * TILE), BF16),
             pltpu.VMEM((3 * tiles, 8, TILE), F32),
             pltpu.VMEM((5, 8, waves), F32),
             pltpu.VMEM((24, waves), BF16),

time: 72.3 us -> 71.1 us (0.983)
  Pallas kernels: 70.6 us -> 69.4 us
    pallas_call x1, Pallas kernels: 70.6 us -> 69.4 us  [body(): pl.pallas_call(functools.partial(kernel, n_space, n_wave), out_shape=jax....]
where the time goes in v4:
time: 71.1 us; the launch traced here: 70.9 us
  Pallas kernels  69.4 us (98%)
  local copies, waits for them, and re-layouts  1.54 us (2%)
    pallas_call x1, Pallas kernels, body(): pl.pallas_call(functools.partial(kernel, n_space, n_wave), out_shape=jax....  69.4 us
    reshape x1, local copies, waits for them, and re-layouts, body(): return jnp.transpose(out, (2, 1, 0, 3)).reshape(vectors, 3, count)  1.54 us

profile of v4, /device:TPU:1, one launch (start us, length us, event | category | flops | bytes accessed | tf_op | source)
XLA Modules:
  0.0 70.9 jit_solution(16846426615393833896)
XLA Ops:
  0.0 69.4 %shard_map.55 = f32[8,24,128]{2,1,0:T(8,128)} custom-call(f32[24,1024]{1,0:T(8,128)} %bitcast.10, f32[3,1024]{1,0:T(4,128)} %pos_hbm.1, s32[3,512]{1,0:T(4,128)} %wave_hbm.1, s32[8,8]{1,0:T(8,128)} %lists_hbm.1, s32[8]{0:T(128)} %counts_hbm.1), custom_call_target="tpu_custom_call" | custom-call | tf_op jit(solution)/shard_map/pallas_call | solution.py:609
  69.4 1.5 %copy_bitcast_fusion = f32[8,3,1024]{2,0,1:T(8,128)} fusion(f32[8,24,128]{2,1,0:T(8,128)} %shard_map.55), kind=kLoop, calls=%fused_computation | loop fusion | bytes 196608 | tf_op jit(solution)/shard_map/reshape | solution.py:667

commit v5 on v4

--- a/solution.py
+++ b/solution.py
@@ -569,11 +569,14 @@
             remote(own, own, wa_s.at[k], wa_r.at[k, d], me, tile_at(d)).start()
         sent.append((whole, n_wave - 1, wa_s.at[k], wa_r.at[k, 0]))
 
-    out_ref[wv] = outb[wv]
+    def put(t):
+        out_ref[:, pl.ds(pl.multiple_of(t * TILE, TILE), TILE)] = outb[t]
+
+    put(wv)
     for d in (1, 7, 2, 6, 3, 5, 4):
         piece = outb.at[tile_at(d)]
         remote(piece, piece, wa_s.at[2], wa_r.at[2, n_wave - d], up, wv).wait_recv()
-        out_ref[tile_at(d)] = outb[tile_at(d)]
+        put(tile_at(d))
     for k in range(DEGREE):
 
         @pl.when(my_c == 0)
@@ -608,7 +611,7 @@
     hbm = pl.BlockSpec(memory_space=pl.ANY)
     out = pl.pallas_call(
         functools.partial(kernel, n_space, n_wave),
-        out_shape=jax.ShapeDtypeStruct((tiles, rows, TILE), F32),
+        out_shape=pltpu.VMEM((rows, count), F32),
         in_specs=[hbm] * 5,
         out_specs=vmem,
         scratch_shapes=[
@@ -663,8 +666,7 @@
             collective_id=0, has_side_effects=True, vmem_limit_bytes=60 * 1024 * 1024
         ),
     )(arranged, positions, wave_index, tile_lists, tile_counts)
-    out = out.reshape(tiles, 3, vectors, TILE)
-    return jnp.transpose(out, (2, 1, 0, 3)).reshape(vectors, 3, count)
+    return jnp.transpose(out.reshape(3, vectors, count), (1, 0, 2))
 
 
 def solution(mesh):

time: 71.1 us -> 69.6 us (0.979)
  local copies, waits for them, and re-layouts: 1.54 us -> 0.64 us
    reshape x1 -> x0, local copies, waits for them, and re-layouts: 1.54 us -> none  [body(): return jnp.transpose(out, (2, 1, 0, 3)).reshape(vectors, 3, count)]
where the time goes in v5:
time: 69.6 us; the launch traced here: 69.4 us
  Pallas kernels  68.8 us (99%)
    pallas_call x1, Pallas kernels, body(): pl.pallas_call(functools.partial(kernel, n_space, n_wave), out_shape=pltp...  68.8 us

profile of v5, /device:TPU:1, one launch (start us, length us, event | category | flops | bytes accessed | tf_op | source)
XLA Modules:
  0.0 69.4 jit_solution(7142781926607785902)
XLA Ops:
  0.0 68.8 %shard_map.55 = f32[24,1024]{1,0:T(8,128)S(1)} custom-call(f32[24,1024]{1,0:T(8,128)} %bitcast.7, f32[3,1024]{1,0:T(4,128)} %pos_hbm.1, s32[3,512]{1,0:T(4,128)} %wave_hbm.1, s32[8,8]{1,0:T(8,128)} %lists_hbm.1, s32[8]{0:T(128)} %counts_hbm.1), custom_call_target="tpu_custom_call" | custom-call | tf_op jit(solution)/shard_map/pallas_call | solution.py:612
  68.8 0.6 copy.7

commit v6 on v5

--- a/solution.py
+++ b/solution.py
@@ -161,7 +161,89 @@
 
     waves = wave_ref.shape[1]
     n_all = wave_ref[...].astype(F32)
-    n_rows = [jnp.broadcast_to(n_all[c : c + 1], (8, waves)) for c in range(3)]
+    padded = jnp.concatenate([n_all, jnp.zeros((5, waves), F32)], axis=0)
+    padded = jnp.concatenate([padded] * 3, axis=0)
+    nf[...] = padded.astype(BF16)
+    for n in range(waves // TILE):
+        at = slice(n * TILE, (n + 1) * TILE)
+        nt[at, :] = jnp.transpose(padded[:, at]).astype(BF16)
+    sides = jnp.where(
+        lax.broadcasted_iota(jnp.int32, (8, TILE), 0) == 0, F32(1.0 / n_space), F32(1.0 / SIDE_CROSS)
+    )
+
+    def trig(angle):
+        r = angle - nearest(angle)
+        r2 = r * r
+        half_sine = polynomial(ODD, r2) * r
+        cosine = 1.0 - half_sine * half_sine
+        sine = half_sine * polynomial(EVEN, r2)
+        halves = []
+        for value in (cosine, sine):
+            high = value.astype(BF16)
+            halves.append((high, (value - high.astype(F32)).astype(BF16)))
+        return halves
+
+    def tile_at(d):
+        return lax.rem(wv + d, n_wave)
+
+    def distance(j):
+        if isinstance(j, int):
+            return (j + 1) // 2 if j % 2 == 1 else (n_wave - j // 2) % n_wave
+        half = lax.div(j + 1, 2)
+        return jnp.where(lax.rem(j, 2) == 1, half, lax.rem(n_wave - half, n_wave))
+
+    def make_phases(t):
+        box = posw[tiles + tile_at(distance(t))] * sides
+        first = box.astype(BF16).astype(F32)
+        second = (box - first).astype(BF16).astype(F32)
+        pieces = jnp.concatenate([first, second, box - first - second], axis=0)
+        pf[:, pl.ds(pl.multiple_of(t * TILE, TILE), TILE)] = pieces.astype(BF16)
+        turns[...] = jnp.dot(
+            jnp.transpose(pieces).astype(BF16), nf[...], preferred_element_type=F32
+        )
+        for j in range(TILE // 16):
+            rows = pl.ds(pl.multiple_of(t * TILE + j * 16, 16), 16)
+            for at, (high, low) in zip((0, waves), trig(turns[j * 16 : (j + 1) * 16])):
+                ph_hi[rows, at : at + waves] = high
+                ph_lo[rows, at : at + waves] = low
+
+    def make_transposed(n, _):
+        block = nt[pl.ds(pl.multiple_of(n * TILE, TILE), TILE), :]
+        turns_t[...] = jnp.dot(block, pf[...], preferred_element_type=F32)
+        for j in range(TILE // 16):
+            for pair in range(tiles // 2):
+                lanes = slice(pair * 2 * TILE, (pair + 1) * 2 * TILE)
+                parts = trig(turns_t[j * 16 : (j + 1) * 16, lanes])
+                for at, (high, low) in zip((0, waves), parts):
+                    rows = pl.ds(pl.multiple_of(at + n * TILE + j * 16, 16), 16)
+                    pt_hi[pair, rows, :] = high
+                    pt_lo[pair, rows, :] = low
+        return 0
+
+    step = 256
+
+    def fold(t):
+        lhs = split_rows(u[0][tiles + tile_at(distance(t))])
+        rows = pl.ds(pl.multiple_of(t * TILE, TILE), TILE)
+        for n in range(2 * waves // step):
+            cols = slice(n * step, (n + 1) * step)
+            c = jnp.dot(lhs, ph_hi[rows, cols], preferred_element_type=F32)
+            c = (c[0:24] + c[24:48]) + jnp.dot(
+                lhs[0:24], ph_lo[rows, cols], preferred_element_type=F32
+            )
+            cacc[:, cols] += c
+
+    def fold_and_make(t, _):
+        fold(t - 1)
+        make_phases(t)
+        return 0
+
+    cacc[...] = jnp.zeros_like(cacc)
+    make_phases(0)
+    for copy in loads[2:]:
+        copy.wait()
+    lax.fori_loop(1, tiles, fold_and_make, 0)
+    n_rows = [jnp.broadcast_to(wave_ref[c : c + 1].astype(F32), (8, waves)) for c in range(3)]
     ka = n_rows[0] * F32(2.0 * math.pi / n_space)
     kb = n_rows[1] * F32(2.0 * math.pi / SIDE_CROSS)
     kc = n_rows[2] * F32(2.0 * math.pi / SIDE_CROSS)
@@ -177,87 +259,6 @@
     ev[2] = -root * ka * kc / (rho * length)
     ev[3] = -root * kb * kc / (rho * length)
     ev[4] = root * rho / length
-    padded = jnp.concatenate([n_all, jnp.zeros((5, waves), F32)], axis=0)
-    padded = jnp.concatenate([padded] * 3, axis=0)
-    nf[...] = padded.astype(BF16)
-    for n in range(waves // TILE):
-        at = slice(n * TILE, (n + 1) * TILE)
-        nt[at, :] = jnp.transpose(padded[:, at]).astype(BF16)
-    sides = jnp.where(
-        lax.broadcasted_iota(jnp.int32, (8, TILE), 0) == 0, F32(1.0 / n_space), F32(1.0 / SIDE_CROSS)
-    )
-
-    def trig(angle):
-        r = angle - nearest(angle)
-        r2 = r * r
-        half_sine = polynomial(ODD, r2) * r
-        cosine = 1.0 - half_sine * half_sine
-        sine = half_sine * polynomial(EVEN, r2)
-        halves = []
-        for value in (cosine, sine):
-            high = value.astype(BF16)
-            halves.append((high, (value - high.astype(F32)).astype(BF16)))
-        return halves
-
-    def tile_at(d):
-        return lax.rem(wv + d, n_wave)
-
-    def distance(j):
-        if isinstance(j, int):
-            return (j + 1) // 2 if j % 2 == 1 else (n_wave - j // 2) % n_wave
-        half = lax.div(j + 1, 2)
-        return jnp.where(lax.rem(j, 2) == 1, half, lax.rem(n_wave - half, n_wave))
-
-    def make_phases(t):
-        box = posw[tiles + tile_at(distance(t))] * sides
-        first = box.astype(BF16).astype(F32)
-        second = (box - first).astype(BF16).astype(F32)
-        pieces = jnp.concatenate([first, second, box - first - second], axis=0)
-        pf[:, pl.ds(pl.multiple_of(t * TILE, TILE), TILE)] = pieces.astype(BF16)
-        turns[...] = jnp.dot(
-            jnp.transpose(pieces).astype(BF16), nf[...], preferred_element_type=F32
-        )
-        for j in range(TILE // 16):
-            rows = pl.ds(pl.multiple_of(t * TILE + j * 16, 16), 16)
-            for at, (high, low) in zip((0, waves), trig(turns[j * 16 : (j + 1) * 16])):
-                ph_hi[rows, at : at + waves] = high
-                ph_lo[rows, at : at + waves] = low
-
-    def make_transposed(n, _):
-        block = nt[pl.ds(pl.multiple_of(n * TILE, TILE), TILE), :]
-        turns_t[...] = jnp.dot(block, pf[...], preferred_element_type=F32)
-        for j in range(TILE // 16):
-            for pair in range(tiles // 2):
-                lanes = slice(pair * 2 * TILE, (pair + 1) * 2 * TILE)
-                parts = trig(turns_t[j * 16 : (j + 1) * 16, lanes])
-                for at, (high, low) in zip((0, waves), parts):
-                    rows = pl.ds(pl.multiple_of(at + n * TILE + j * 16, 16), 16)
-                    pt_hi[pair, rows, :] = high
-                    pt_lo[pair, rows, :] = low
-        return 0
-
-    step = 256
-
-    def fold(t):
-        lhs = split_rows(u[0][tiles + tile_at(distance(t))])
-        rows = pl.ds(pl.multiple_of(t * TILE, TILE), TILE)
-        for n in range(2 * waves // step):
-            cols = slice(n * step, (n + 1) * step)
-            c = jnp.dot(lhs, ph_hi[rows, cols], preferred_element_type=F32) + jnp.dot(
-                lhs, ph_lo[rows, cols], preferred_element_type=F32
-            )
-            cacc[:, cols] += c[0:24] + c[24:48]
-
-    def fold_and_make(t, _):
-        fold(t - 1)
-        make_phases(t)
-        return 0
-
-    cacc[...] = jnp.zeros_like(cacc)
-    make_phases(0)
-    for copy in loads[2:]:
-        copy.wait()
-    lax.fori_loop(1, tiles, fold_and_make, 0)
     fold(tiles - 1)
 
     def halo(k):
@@ -376,13 +377,14 @@
             rows = slice(group[0] * TILE, (group[-1] + 1) * TILE)
             for n in range(2 * waves // step):
                 cols = slice(n * step, (n + 1) * step)
-                c = jnp.dot(lhs, ph_hi[rows, cols], preferred_element_type=F32) + jnp.dot(
-                    lhs, ph_lo[rows, cols], preferred_element_type=F32
+                c = jnp.dot(lhs, ph_hi[rows, cols], preferred_element_type=F32)
+                c = (c[0:24] + c[24:48]) + jnp.dot(
+                    lhs[0:24], ph_lo[rows, cols], preferred_element_type=F32
                 )
                 if group[0] == 0:
-                    cacc[:, cols] = c[0:24] + c[24:48]
+                    cacc[:, cols] = c
                 else:
-                    cacc[:, cols] += c[0:24] + c[24:48]
+                    cacc[:, cols] += c
         for n in range(waves // step):
             for half in range(2):
                 c = cacc[:, half * waves + n * step : half * waves + (n + 1) * step]
@@ -487,10 +489,10 @@
 
         def back_pair(i, _):
             pair = tiles // 2 - 1 - i
-            v = jnp.dot(back[...], pt_hi[pair], preferred_element_type=F32) + jnp.dot(
-                back[...], pt_lo[pair], preferred_element_type=F32
+            v = jnp.dot(back[...], pt_hi[pair], preferred_element_type=F32)
+            v = (v[0:24] + v[24:48]) + jnp.dot(
+                back[0:24, :], pt_lo[pair], preferred_element_type=F32
             )
-            v = v[0:24] + v[24:48]
 
             def part(d, q):
                 t = tile_at(d)

time: 69.6 us -> 69.6 us (level)
  no operation moved by 1% of the time
where the time goes in v6:
time: 69.6 us; the launch traced here: 69.4 us
  Pallas kernels  68.8 us (99%)
    pallas_call x1, Pallas kernels, body(): pl.pallas_call(functools.partial(kernel, n_space, n_wave), out_shape=pltp...  68.8 us

profile of v6, /device:TPU:1, one launch (start us, length us, event | category | flops | bytes accessed | tf_op | source)
XLA Modules:
  0.0 69.4 jit_solution(4501270582611610853)
XLA Ops:
  0.0 68.8 %shard_map.55 = f32[24,1024]{1,0:T(8,128)S(1)} custom-call(f32[24,1024]{1,0:T(8,128)} %bitcast.7, f32[3,1024]{1,0:T(4,128)} %pos_hbm.1, s32[3,512]{1,0:T(4,128)} %wave_hbm.1, s32[8,8]{1,0:T(8,128)} %lists_hbm.1, s32[8]{0:T(128)} %counts_hbm.1), custom_call_target="tpu_custom_call" | custom-call | tf_op jit(solution)/shard_map/pallas_call | solution.py:614
  68.8 0.6 copy.7

commit v7 on v6

--- a/solution.py
+++ b/solution.py
@@ -125,20 +125,12 @@
 
     barrier = pltpu.get_barrier_semaphore()
 
-    def greet_space(d, _):
-        pl.semaphore_signal(
-            barrier, inc=1, device_id=(lax.rem(me + d, n_space), wv), device_id_type=MESH
-        )
-        return 0
-
-    def greet_wave(d, _):
-        pl.semaphore_signal(
-            barrier, inc=1, device_id=(me, lax.rem(wv + d, n_wave)), device_id_type=MESH
-        )
-        return 0
-
-    lax.fori_loop(1, n_space, greet_space, 0)
-    lax.fori_loop(1, n_wave, greet_wave, 0)
+    ring = (0, 1, 2, 1)
+    greeted = sorted(range(1, n_space), key=lambda d: -(ring[d // 8] + ring[d // 2 % 4]))
+    peers = [(lax.rem(me + d, n_space), wv) for d in greeted]
+    peers = [(me, lax.rem(wv + d, n_wave)) for d in (4, 3, 5, 2, 6, 1, 7)] + peers
+    for peer in peers:
+        pl.semaphore_signal(barrier, inc=1, device_id=peer, device_id_type=MESH)
 
     def remote(src, dst, ssem, rsem, s, w):
         return pltpu.make_async_remote_copy(

time: 69.6 us -> 69.3 us (level)
  no operation moved by 1% of the time
where the time goes in v7:
time: 69.3 us; the launch traced here: 69 us
  Pallas kernels  68.4 us (99%)
    pallas_call x1, Pallas kernels, body(): pl.pallas_call(functools.partial(kernel, n_space, n_wave), out_shape=pltp...  68.4 us

profile of v7, /device:TPU:1, one launch (start us, length us, event | category | flops | bytes accessed | tf_op | source)
XLA Modules:
  0.0 69.0 jit_solution(15509218708356931285)
XLA Ops:
  0.0 68.4 %shard_map.55 = f32[24,1024]{1,0:T(8,128)S(1)} custom-call(f32[24,1024]{1,0:T(8,128)} %bitcast.7, f32[3,1024]{1,0:T(4,128)} %pos_hbm.1, s32[3,512]{1,0:T(4,128)} %wave_hbm.1, s32[8,8]{1,0:T(8,128)} %lists_hbm.1, s32[8]{0:T(128)} %counts_hbm.1), custom_call_target="tpu_custom_call" | custom-call | tf_op jit(solution)/shard_map/pallas_call | solution.py:606
  68.4 0.6 copy.7
